TPU v7x, 256 devices: a whole 4x4x8 slice. The times are simulated.
256 devices in a mesh: ens: 8 (over z), dom: 32 (over y, x, core).
Axes of the slice: x: 4, y: 4, z: 8, core: 2. Of those that a mesh axis runs over, the one named last changes fastest.
Arguments:
- state: float32 [256, 1024, 128], P('ens', 'dom'), may hold values from -6 to 6
- row_courant: float32 [1024, 128], P('dom'), may hold values from 0.3 to 0.6
- col_courant: float32 [1024, 128], P('dom'), may hold values from 0.05 to 0.2
- diffusion: float32 [1024, 128], P('dom'), may hold values from 0.01 to 0.05
- obs_values: float32 [4, 256], replicated, may hold values from -8 to 8
- obs_variance: float32 [4, 256], replicated, may hold values from 0.25 to 4
- obs_offsets: int32 [4, 256], replicated, may hold values from 0 to 4095
- owners: int32 [4], replicated, may hold values from 0 to 31, as said below
Outputs:
- analysis: float32 [256, 1024, 128], P('ens', 'dom')
Inputs may be any that keep to these rules, and one draw needn't show every extreme that they name: `owners`: distinct domain blocks, one for each batch.
All inputs are finite; a program needn't handle non-finite values.
Results may differ from a plain program's by a relative error of at most 0.0002.
Values sent between devices are 32-bit elements; how exact they have to be, the bound alone decides.
A program may use at most 64 MiB of HBM per device.

v0:
```python
import functools

import jax
import jax.numpy as jnp
from jax import lax
from jax.sharding import Mesh
from jax.sharding import PartitionSpec as P

FSTEPS = 4
DOM = ("dom_0", "dom_1", "dom_2")
ENS_DOM = ("ens", "dom_0", "dom_1", "dom_2")


def with_halo(x, sides, width):
    for axis, dim in sides:
        devices, length = (lax.axis_size(axis), x.shape[dim])
        up = [(i, (i + 1) % devices) for i in range(devices)]
        down = [(j, i) for i, j in up]
        last = lax.slice_in_dim(x, length - width, length, axis=dim)
        leading = lax.slice_in_dim(x, 0, width, axis=dim)
        before = lax.ppermute(last, axis, up)
        after = lax.ppermute(leading, axis, down)
        x = jnp.concatenate([before, x, after], axis=dim)
    return x


def over_axes(x, axes):
    return functools.reduce(lax.psum, axes, x)


def advance_rows(padded, coef):
    center = padded[:, 1:-1]
    upper = padded[:, :-2]
    lower = padded[:, 2:]
    left = jnp.roll(center, 1, axis=2)
    right = jnp.roll(center, -1, axis=2)
    inner = coef[:, 1:-1]
    row_c = inner[0][None]
    col_c = inner[1][None]
    diff_c = inner[2][None]
    fresh = (
        center
        - row_c * (center - upper)
        - col_c * (center - left)
        + diff_c * (upper + lower + left + right - 4.0 * center)
    )
    return (fresh, inner)


def contract_members(left_side, right_side):
    return lax.dot_general(
        left_side,
        right_side,
        (((0,), (0,)), ((), ())),
        precision=lax.Precision.HIGHEST,
        preferred_element_type=jnp.float32,
    )


def on_device(
    state, row_courant, col_courant, diffusion, obs_values, obs_variance, obs_offsets, owners
):
    mem_count, rows_dev, cols = state.shape
    coefs = jnp.stack([row_courant, col_courant, diffusion])
    field = state
    for step in range(FSTEPS):
        padded = with_halo(jnp.concatenate([field, coefs], axis=0), ((DOM, 1),), 1)
        field, unused = advance_rows(padded[:mem_count], padded[mem_count:])
    regrouped = lax.all_to_all(field, "ens", split_axis=1, concat_axis=0, tiled=True)
    members, sub_rows, unused_cols = regrouped.shape
    local_cells = sub_rows * cols
    matrix = regrouped.reshape(members, local_cells)
    base = (lax.axis_index(DOM) * rows_dev + lax.axis_index("ens") * sub_rows) * cols
    scale = 1.0 / (members - 1.0)

    def fetch(matrix, batch):
        cells = owners[batch] * (rows_dev * cols) + obs_offsets[batch]
        local = cells - base
        inside = (local >= 0) & (local < local_cells)
        picked = jnp.take(matrix, jnp.clip(local, 0, local_cells - 1), axis=1)
        values = jnp.where(inside[None, :], picked, 0.0)
        return over_axes(values, ENS_DOM)

    batches = obs_values.shape[0]
    priors = [fetch(matrix, batch) for batch in range(batches)]
    for batch in range(batches):
        observed = priors[batch]
        ybar = jnp.mean(observed, axis=0)
        anom_obs = observed - ybar
        system = contract_members(anom_obs, anom_obs) * scale + jnp.diag(obs_variance[batch])
        factor = jnp.linalg.cholesky(system)
        target = (obs_values[batch] - ybar)[None, :] - 0.5 * anom_obs
        weights = jax.scipy.linalg.cho_solve((factor, True), target.T).T
        anomaly = matrix - jnp.mean(matrix, axis=0)
        spread = contract_members(anom_obs, anomaly) * scale
        updated = matrix + jnp.dot(weights, spread, precision=lax.Precision.HIGHEST)
        matrix, weights, anom_obs = (updated, weights, anom_obs)
        for later in range(batch + 1, batches):
            column = priors[later]
            centered = column - jnp.mean(column, axis=0)
            shift_obs = contract_members(anom_obs, centered) * scale
            priors[later] = column + jnp.dot(weights, shift_obs, precision=lax.Precision.HIGHEST)
    back = matrix.reshape(members, sub_rows, cols)
    return lax.all_to_all(back, "ens", split_axis=0, concat_axis=1, tiled=True)


def solution(mesh):
    finer = Mesh(
        mesh.devices.reshape(mesh.shape["ens"], 4, 4, 2), ("ens", "dom_0", "dom_1", "dom_2")
    )
    return jax.shard_map(
        on_device,
        mesh=finer,
        in_specs=(
            P("ens", DOM, None),
            P(DOM, None),
            P(DOM, None),
            P(DOM, None),
            P(),
            P(),
            P(),
            P(),
        ),
        out_specs=P("ens", DOM, None),
        check_vma=False,
    )
```

profile of v0, /device:TPU:1, one launch (start us, length us, event | category | flops | bytes accessed | tf_op | source)
XLA Modules:
  0.0 594.2 jit_solution(14678740836794500095)
XLA Ops:
  6.5 1.4 copy.31
  8.0 2.7 collective-permute-start
  10.7 0.7 collective-permute-start.1
  12.5 0.7 fusion.174
  15.8 0.7 copy-done.8
  17.4 1.1 collective-permute-start.2
  18.5 4.0 collective-permute-start.3
  24.4 5.7 collective-permute-start.5
  31.9 5.8 collective-permute-start.7
  38.5 1.3 fusion.35
  39.8 6.5 %all-to-all-start = ((f32[32,32,128]{2,0,1:T(8,128)}), f32[32,32,128]{2,0,1:T(8,128)S(1)}, u32[]{:S(2)}, u32[]{:S(2)}) async-start(f32[32,32,128]{2,0,1:T(8,128)} %fusion.35), calls=%async_computation | async-start | bytes 1048576 | tf_op jit(solution)/shard_map/all_to_all | solution.py:69
  46.6 11.9 %all-to-all-done = f32[32,32,128]{2,0,1:T(8,128)S(1)} async-done(((f32[32,32,128]{2,0,1:T(8,128)}), f32[32,32,128]{2,0,1:T(8,128)S(1)}, u32[]{:S(2)}, u32[]{:S(2)}) %all-to-all-start) | async-done | bytes 524320 | tf_op jit(solution)/shard_map/all_to_all | solution.py:69
  59.2 1.0 gather_fusion.3
  60.1 1.0 gather_fusion.2
  61.1 1.0 gather_fusion.1
  62.1 1.0 gather_fusion
  63.0 0.8 bitcast_select_fusion
  63.9 0.8 bitcast_select_fusion.1
  64.7 0.8 bitcast_select_fusion.2
  65.5 0.8 bitcast_select_fusion.3
  66.5 74.3 %all-reduce.10.cloned.1.call-done = (f32[256,256]{0,1:T(8,128)}, f32[256,256]{0,1:T(8,128)}, f32[256,256]{0,1:T(8,128)}, f32[256,256]{0,1:T(8,128)}) async-done(((f32[256,256]{0,1:T(8,128)}, f32[256,256]{0,1:T(8,128)}, f32[256,256]{0,1:T(8,128)}, f32[256,256]{0,1:T(8,128)}), (f32[256,256]{0,1:T(8,128)}, f32[256,256]{0,1:T(8,128)}, f32[256,256]{0,1:T(8,128)}, ...) | async-done | bytes 1048592 | tf_op jit(solution)/shard_map/psum | solution.py:28
  140.9 55.4 %all-reduce.14.cloned.1.call-done = (f32[256,256]{0,1:T(8,128)}, f32[256,256]{0,1:T(8,128)}, f32[256,256]{0,1:T(8,128)}, f32[256,256]{0,1:T(8,128)}) async-done(((f32[256,256]{0,1:T(8,128)}, f32[256,256]{0,1:T(8,128)}, f32[256,256]{0,1:T(8,128)}, f32[256,256]{0,1:T(8,128)}), (f32[256,256]{0,1:T(8,128)}, f32[256,256]{0,1:T(8,128)}, f32[256,256]{0,1:T(8,128)}, ...) | async-done | bytes 1048592 | tf_op jit(solution)/shard_map/psum | solution.py:28
  196.3 54.7 %all-reduce.12.cloned.1.call-done = (f32[256,256]{0,1:T(8,128)}, f32[256,256]{0,1:T(8,128)}, f32[256,256]{0,1:T(8,128)}, f32[256,256]{0,1:T(8,128)}) async-done(((f32[256,256]{0,1:T(8,128)}, f32[256,256]{0,1:T(8,128)}, f32[256,256]{0,1:T(8,128)}, f32[256,256]{0,1:T(8,128)}), (f32[256,256]{0,1:T(8,128)}, f32[256,256]{0,1:T(8,128)}, f32[256,256]{0,1:T(8,128)}, ...) | async-done | bytes 1048592 | tf_op jit(solution)/shard_map/psum | solution.py:28
  251.1 0.7 copy-done.10
  252.1 35.4 %all-reduce.16.cloned.1.call-done = (f32[256,256]{0,1:T(8,128)}, f32[256,256]{0,1:T(8,128)}, f32[256,256]{0,1:T(8,128)}, f32[256,256]{0,1:T(8,128)}) async-done(((f32[256,256]{0,1:T(8,128)}, f32[256,256]{0,1:T(8,128)}, f32[256,256]{0,1:T(8,128)}, f32[256,256]{0,1:T(8,128)}), (f32[256,256]{0,1:T(8,128)}, f32[256,256]{0,1:T(8,128)}, f32[256,256]{0,1:T(8,128)}, ...) | async-done | bytes 1048592 | tf_op jit(solution)/shard_map/psum | solution.py:28
  287.5 1.1 reduce_sum.126
  290.0 11.7 %cholesky.214 = f32[128,128]{1,0:T(8,128)S(1)} custom-call(f32[128,128]{1,0:T(8,128)S(1)} %cholesky.346), custom_call_target="Cholesky" | custom-call | tf_op jit(solution)/shard_map/jit(cholesky)/cholesky | solution.py:91
  301.8 9.8 %custom-call.19 = f32[1,128,128]{1,2,0:T(8,128)S(1)} custom-call(f32[1,128,128]{2,1,0:T(8,128)S(1)} %get-tuple-element.141), custom_call_target="InvertDiagBlocksLowerTriangular" | custom-call | tf_op jit(solution)/shard_map/jit(cholesky)/cholesky | solution.py:91
  312.1 11.7 %cholesky.231 = f32[128,128]{1,0:T(8,128)S(1)} custom-call(f32[128,128]{1,0:T(8,128)S(1)} %convolution_subtract_fusion.11), custom_call_target="Cholesky" | custom-call | tf_op jit(solution)/shard_map/jit(cholesky)/cholesky | solution.py:91
  324.5 0.7 compare_reduce_fusion.7
  326.6 4.1 while.8
  326.6 0.7 fusion.226
  327.3 1.3 bitcast_dynamic-update-slice_fusion.8
  328.6 0.7 fusion.226
  329.3 1.3 bitcast_dynamic-update-slice_fusion.8
  330.7 28.4 %custom-call.20 = f32[2,128,128]{1,2,0:T(8,128)S(1)} custom-call(f32[2,128,128]{2,1,0:T(8,128)S(1)} %get-tuple-element.34), custom_call_target="InvertDiagBlocksLowerTriangular" | custom-call | tf_op jit(solution)/shard_map/jit(_cho_solve)/triangular_solve | solution.py:93
  363.8 11.7 %cholesky.248 = f32[128,128]{1,0:T(8,128)S(1)} custom-call(f32[128,128]{1,0:T(8,128)S(1)} %cholesky.349), custom_call_target="Cholesky" | custom-call | tf_op jit(solution)/shard_map/jit(cholesky)/cholesky | solution.py:91
  375.6 9.8 %custom-call.21 = f32[1,128,128]{1,2,0:T(8,128)S(1)} custom-call(f32[1,128,128]{2,1,0:T(8,128)S(1)} %get-tuple-element.137), custom_call_target="InvertDiagBlocksLowerTriangular" | custom-call | tf_op jit(solution)/shard_map/jit(cholesky)/cholesky | solution.py:91
  385.8 12.1 %cholesky.265 = f32[128,128]{1,0:T(8,128)S(1)} custom-call(f32[128,128]{1,0:T(8,128)S(1)} %convolution_subtract_fusion.10), custom_call_target="Cholesky" | custom-call | tf_op jit(solution)/shard_map/jit(cholesky)/cholesky | solution.py:91
  398.7 0.7 compare_reduce_fusion.5
  400.7 4.0 while.9
  401.3 1.3 bitcast_dynamic-update-slice_fusion.9
  403.4 1.3 bitcast_dynamic-update-slice_fusion.9
  404.7 19.7 %custom-call.22 = f32[2,128,128]{1,2,0:T(8,128)S(1)} custom-call(f32[2,128,128]{2,1,0:T(8,128)S(1)} %get-tuple-element.35), custom_call_target="InvertDiagBlocksLowerTriangular" | custom-call | tf_op jit(solution)/shard_map/jit(_cho_solve)/triangular_solve | solution.py:93
  430.6 11.7 %cholesky.282 = f32[128,128]{1,0:T(8,128)S(1)} custom-call(f32[128,128]{1,0:T(8,128)S(1)} %cholesky.352), custom_call_target="Cholesky" | custom-call | tf_op jit(solution)/shard_map/jit(cholesky)/cholesky | solution.py:91
  442.3 9.8 %custom-call.23 = f32[1,128,128]{1,2,0:T(8,128)S(1)} custom-call(f32[1,128,128]{2,1,0:T(8,128)S(1)} %get-tuple-element.133), custom_call_target="InvertDiagBlocksLowerTriangular" | custom-call | tf_op jit(solution)/shard_map/jit(cholesky)/cholesky | solution.py:91
  452.6 11.9 %cholesky.299 = f32[128,128]{1,0:T(8,128)S(1)} custom-call(f32[128,128]{1,0:T(8,128)S(1)} %convolution_subtract_fusion.9), custom_call_target="Cholesky" | custom-call | tf_op jit(solution)/shard_map/jit(cholesky)/cholesky | solution.py:91
  465.2 0.7 compare_reduce_fusion.3
  467.2 4.1 while.10
  467.2 0.7 fusion.228
  467.9 1.3 bitcast_dynamic-update-slice_fusion.10
  469.3 0.7 fusion.228
  469.9 1.3 bitcast_dynamic-update-slice_fusion.10
  471.3 19.7 %custom-call.24 = f32[2,128,128]{1,2,0:T(8,128)S(1)} custom-call(f32[2,128,128]{2,1,0:T(8,128)S(1)} %get-tuple-element.36), custom_call_target="InvertDiagBlocksLowerTriangular" | custom-call | tf_op jit(solution)/shard_map/jit(_cho_solve)/triangular_solve | solution.py:93
  494.5 11.7 %cholesky.316 = f32[128,128]{1,0:T(8,128)S(1)} custom-call(f32[128,128]{1,0:T(8,128)S(1)} %cholesky.355), custom_call_target="Cholesky" | custom-call | tf_op jit(solution)/shard_map/jit(cholesky)/cholesky | solution.py:91
  506.3 9.8 %custom-call.25 = f32[1,128,128]{1,2,0:T(8,128)S(1)} custom-call(f32[1,128,128]{2,1,0:T(8,128)S(1)} %get-tuple-element.129), custom_call_target="InvertDiagBlocksLowerTriangular" | custom-call | tf_op jit(solution)/shard_map/jit(cholesky)/cholesky | solution.py:91
  516.6 11.9 %cholesky.333 = f32[128,128]{1,0:T(8,128)S(1)} custom-call(f32[128,128]{1,0:T(8,128)S(1)} %convolution_subtract_fusion.8), custom_call_target="Cholesky" | custom-call | tf_op jit(solution)/shard_map/jit(cholesky)/cholesky | solution.py:91
  529.2 0.7 compare_reduce_fusion.1
  531.2 4.1 while.11
  531.9 1.3 bitcast_dynamic-update-slice_fusion.11
  533.9 1.3 bitcast_dynamic-update-slice_fusion.11
  535.3 19.7 %custom-call.26 = f32[2,128,128]{1,2,0:T(8,128)S(1)} custom-call(f32[2,128,128]{2,1,0:T(8,128)S(1)} %get-tuple-element.37), custom_call_target="InvertDiagBlocksLowerTriangular" | custom-call | tf_op jit(solution)/shard_map/jit(_cho_solve)/triangular_solve | solution.py:93
  562.3 24.1 %all_to_all.33 = f32[256,4,128]{2,1,0:T(4,128)S(1)} all-to-all(f32[256,4,128]{2,1,0:T(4,128)S(1)} %reshape.164), channel_id=1, replica_groups=mesh['ens'=8,'dom_0'=4,'dom_1'=4,'dom_2'=2] {'ens'}, dimensions={0} | all-to-all | bytes 1048576 | tf_op jit(solution)/shard_map/all_to_all | solution.py:104
  586.4 0.9 copy.57
  (207 shorter events, 38.1 us)
Async XLA Ops:
  6.5 1.4 copy-start.1
  6.5 1.4 copy-start.2
  6.5 1.4 copy-start.3
  8.0 8.5 %collective-permute-start = (f32[35,1,128]{2,0,1:T(8,128)S(1)}, f32[35,1,128]{2,0,1:T(8,128)S(1)}, u32[]{:S(2)}, u32[]{:S(2)}) collective-permute-start(f32[35,1,128]{2,0,1:T(8,128)S(1)} %get-tuple-element.108), channel_id=1, source_target_pairs={{0,1},{1,2},{2,3},{3,4},{4,5},{5,6},{6,7},{7,8},{8,9},{9,10},{10,1... | collective-permute-start | bytes 53768 | tf_op jit(solution)/shard_map/ppermute | solution.py:21
  10.7 5.9 collective-permute-start.1
  11.8 0.7 copy-start.7
  15.8 0.7 copy-start.8
  17.4 5.7 collective-permute-start.2
  18.5 4.9 collective-permute-start.3
  24.3 6.4 %collective-permute-start.4 = (f32[35,1,128]{2,0,1:T(8,128)S(1)}, f32[35,1,128]{2,0,1:T(8,128)S(1)}, u32[]{:S(2)}, u32[]{:S(2)}) collective-permute-start(f32[35,1,128]{2,0,1:T(8,128)S(1)} %get-tuple-element.104), channel_id=1, source_target_pairs={{0,1},{1,2},{2,3},{3,4},{4,5},{5,6},{6,7},{7,8},{8,9},{9,10},{10,1... | collective-permute-start | bytes 53768 | tf_op jit(solution)/shard_map/ppermute | solution.py:21
  24.4 6.5 %collective-permute-start.5 = (f32[35,1,128]{2,0,1:T(8,128)S(1)}, f32[35,1,128]{2,0,1:T(8,128)S(1)}, u32[]{:S(2)}, u32[]{:S(2)}) collective-permute-start(f32[35,1,128]{2,0,1:T(8,128)S(1)} %get-tuple-element.105), channel_id=1, source_target_pairs={{1,0},{2,1},{3,2},{4,3},{5,4},{6,5},{7,6},{8,7},{9,8},{10,9},{11,1... | collective-permute-start | bytes 53768 | tf_op jit(solution)/shard_map/ppermute | solution.py:22
  31.8 6.4 %collective-permute-start.6 = (f32[35,1,128]{2,0,1:T(8,128)S(1)}, f32[35,1,128]{2,0,1:T(8,128)S(1)}, u32[]{:S(2)}, u32[]{:S(2)}) collective-permute-start(f32[35,1,128]{2,0,1:T(8,128)S(1)} %get-tuple-element.102), channel_id=1, source_target_pairs={{0,1},{1,2},{2,3},{3,4},{4,5},{5,6},{6,7},{7,8},{8,9},{9,10},{10,1... | collective-permute-start | bytes 53768 | tf_op jit(solution)/shard_map/ppermute | solution.py:21
  31.9 6.6 %collective-permute-start.7 = (f32[35,1,128]{2,0,1:T(8,128)S(1)}, f32[35,1,128]{2,0,1:T(8,128)S(1)}, u32[]{:S(2)}, u32[]{:S(2)}) collective-permute-start(f32[35,1,128]{2,0,1:T(8,128)S(1)} %get-tuple-element.103), channel_id=1, source_target_pairs={{1,0},{2,1},{3,2},{4,3},{5,4},{6,5},{7,6},{8,7},{9,8},{10,9},{11,1... | collective-permute-start | bytes 53768 | tf_op jit(solution)/shard_map/ppermute | solution.py:22
  39.8 18.8 %all-to-all-start = ((f32[32,32,128]{2,0,1:T(8,128)}), f32[32,32,128]{2,0,1:T(8,128)S(1)}, u32[]{:S(2)}, u32[]{:S(2)}) async-start(f32[32,32,128]{2,0,1:T(8,128)} %fusion.35), calls=%async_computation | async-start | bytes 1048576 | tf_op jit(solution)/shard_map/all_to_all | solution.py:69
  46.3 94.5 %all-reduce.10.cloned.1.call-start = ((), (), s32[]{:S(2)}) async-start(), calls=%async_computation.2 | async-start | bytes 2097152 | tf_op jit(solution)/shard_map/psum | solution.py:28
  66.4 129.8 %all-reduce.14.cloned.1.call-start = ((), (), s32[]{:S(2)}) async-start(), calls=%async_computation.4 | async-start | bytes 2097152 | tf_op jit(solution)/shard_map/psum | solution.py:28
  140.8 110.2 %all-reduce.12.cloned.1.call-start = ((), (), s32[]{:S(2)}) async-start(), calls=%async_computation.3 | async-start | bytes 2097152 | tf_op jit(solution)/shard_map/psum | solution.py:28
  196.3 91.2 %all-reduce.16.cloned.1.call-start = ((), (), s32[]{:S(2)}) async-start(), calls=%async_computation.5 | async-start | bytes 2097152 | tf_op jit(solution)/shard_map/psum | solution.py:28
  251.1 0.7 copy-start.10
  287.5 1.2 copy-start.6
  287.5 1.3 copy-start
  330.7 28.4 %copy-start.9 = (f32[4,256]{1,0:T(4,128)S(1)}, f32[4,256]{1,0:T(4,128)}, u32[]{:S(2)}) copy-start(f32[4,256]{1,0:T(4,128)} %param.17) | copy-start | bytes 12292
  361.0 1.0 copy-start.5
  426.8 1.0 copy-start.4
Sparse Core Ops, SparseCore 0:
  66.5 74.2 all-reduce.9
  143.4 52.8 all-reduce.13
  198.8 52.1 all-reduce.11
  253.7 33.7 all-reduce.15
where the time goes:
time: 602 us; the launch traced here: 594 us
  other arithmetic  236 us (39%)
  waiting for transfers between devices  234 us (39%)
  local copies, waits for them, and re-layouts  29 us (5%)
  starting transfers between devices  27 us (4%)
  blocking collectives  24.1 us (4%)
  between operations  22.3 us (4%)
  matrix products  21.7 us (4%)
    psum x4, waiting for transfers between devices, over_axes(): return functools.reduce(lax.psum, axes, x)  220 us
    another operation x28, other arithmetic, on_device(): factor = jnp.linalg.cholesky(system)  139 us
    another operation x9, other arithmetic, on_device(): weights = jax.scipy.linalg.cho_solve((factor, True), target.T).T  87.6 us
    all_to_all x1, blocking collectives, on_device(): return lax.all_to_all(back, 'ens', split_axis=0, concat_axis=1, tiled=True)  24.1 us
    another operation x29, local copies, waits for them, and re-layouts, on_device(): weights = jax.scipy.linalg.cho_solve((factor, True), target.T).T  16.2 us
    ppermute x4, starting transfers between devices, with_halo(): after = lax.ppermute(leading, axis, down)  16.2 us
  transfers between devices with their start and end apart: 13, of which 11 were waited for; matrix products, arithmetic and copies ran while one was open for 0% of the time, Pallas kernels for 0%

commit v1 on v0

v1 whole, which is shorter than its diff:
```python
import functools

import jax
import jax.numpy as jnp
from jax import lax
from jax.experimental import pallas as pl
from jax.experimental.pallas import tpu as pltpu
from jax.sharding import PartitionSpec as P

MESH = pl.DeviceIdType.MESH
FSTEPS = 4
HALO = 8
PAD = 8
HIGHEST = lax.Precision.HIGHEST


def dot(a, b, precision=HIGHEST):
    return jnp.dot(a, b, precision=precision, preferred_element_type=jnp.float32)


def dot_nt(a, b):
    return lax.dot_general(
        a, b, (((1,), (1,)), ((), ())), precision=HIGHEST, preferred_element_type=jnp.float32
    )


def split2(x):
    hi = x.astype(jnp.bfloat16)
    lo = (x - hi.astype(jnp.float32)).astype(jnp.bfloat16)
    return hi, lo


def split3(x):
    hi = x.astype(jnp.bfloat16)
    rest = x - hi.astype(jnp.float32)
    mid = rest.astype(jnp.bfloat16)
    lo = (rest - mid.astype(jnp.float32)).astype(jnp.bfloat16)
    return hi, mid, lo


def bdot(a, b):
    return jnp.dot(a, b, preferred_element_type=jnp.float32)


def kernel(
    state, row_c, col_c, diff, obs, var, off, own_v, own_s, out,
    ext, cext, full, lane_hot, row_hot, hx, a_in, b_out, c_src, arrived, prior, pair,
    total, t_own, load_sem, h_send, h_recv, a_send, a_recv, b_send, b_recv,
    c_send, c_recv, g_send, g_recv,
):
    ens_n = lax.axis_size("ens")
    dom_n = lax.axis_size("dom")
    e = lax.axis_index("ens")
    d = lax.axis_index("dom")
    mem_loc, rows_dev, cols = state.shape
    members = mem_loc * ens_n
    nb, nob = obs.shape
    parts = nob // cols

    loads = [
        pltpu.make_async_copy(state, ext.at[:, pl.ds(HALO, rows_dev), :], load_sem.at[0])
    ]
    for i, coef in enumerate((row_c, col_c, diff)):
        loads.append(
            pltpu.make_async_copy(coef, cext.at[i, pl.ds(HALO, rows_dev), :], load_sem.at[1 + i])
        )
    for copy in loads:
        copy.start()

    barrier = pltpu.get_barrier_semaphore()

    def greet_dom(i, carry):
        pl.semaphore_signal(
            barrier, inc=1, device_id=(e, lax.rem(d + i, dom_n)), device_id_type=MESH
        )
        return carry

    def greet_ens(i, carry):
        pl.semaphore_signal(
            barrier, inc=1, device_id=(lax.rem(e + i, ens_n), d), device_id_type=MESH
        )
        return carry

    lax.fori_loop(1, dom_n, greet_dom, 0)
    lax.fori_loop(1, ens_n, greet_ens, 0)
    pl.semaphore_wait(barrier, dom_n - 1 + ens_n - 1)

    down = lax.rem(d + 1, dom_n)
    up = lax.rem(d + dom_n - 1, dom_n)
    halos = []
    for way, (src_row, dst_row, peer) in enumerate(
        ((rows_dev - HALO, 0, down), (0, HALO + rows_dev, up))
    ):
        halos.append(
            pltpu.make_async_remote_copy(
                src_ref=state.at[:, pl.ds(src_row, HALO), :],
                dst_ref=ext.at[:, pl.ds(dst_row, HALO), :],
                send_sem=h_send.at[way * 4],
                recv_sem=h_recv.at[way * 4],
                device_id=(e, peer),
                device_id_type=MESH,
            )
        )
        for i, coef in enumerate((row_c, col_c, diff)):
            halos.append(
                pltpu.make_async_remote_copy(
                    src_ref=coef.at[pl.ds(src_row, HALO), :],
                    dst_ref=cext.at[i, pl.ds(dst_row, HALO), :],
                    send_sem=h_send.at[way * 4 + 1 + i],
                    recv_sem=h_recv.at[way * 4 + 1 + i],
                    device_id=(e, peer),
                    device_id_type=MESH,
                )
            )
    for copy in halos:
        copy.start()

    mine = (own_v[...] == d).astype(jnp.int32)
    offs = jnp.sum(off[...] * mine, axis=0, keepdims=True)
    lane_of = lax.rem(offs, cols)
    row_of = lax.div(offs, cols)
    lane_hot[...] = (
        lax.broadcasted_iota(jnp.int32, (cols, nob), 0) == lane_of
    ).astype(jnp.float32).astype(jnp.bfloat16)
    row_hot[...] = (
        lax.broadcasted_iota(jnp.int32, (rows_dev, nob), 0) == row_of
    ).astype(jnp.float32)

    for copy in loads:
        copy.wait()
    for copy in halos:
        copy.wait_recv()

    high = rows_dev + 2 * HALO
    rc, cc, df = cext[0], cext[1], cext[2]
    w_up = rc + df
    w_left = cc + df
    w_mid = 1.0 - rc - cc - 4.0 * df
    group = 2

    def forecast(i, carry):
        fields = []
        for j in range(group):
            m = i * group + j
            x = ext[m]
            for _ in range(FSTEPS):
                above = pltpu.roll(x, 1, 0)
                below = pltpu.roll(x, high - 1, 0)
                left = pltpu.roll(x, 1, 1)
                right = pltpu.roll(x, cols - 1, 1)
                x = w_mid * x + w_up * above + w_left * left + df * (below + right)
            x = x[HALO : HALO + rows_dev]
            full[e, pl.ds(m, rows_dev, stride=mem_loc), :] = x
            fields.append(x)
        hi, mid, lo = split3(jnp.concatenate(fields, axis=0))
        hot = lane_hot[...]
        picked = bdot(hi, hot) + bdot(mid, hot) + bdot(lo, hot)
        for j in range(group):
            part = picked[j * rows_dev : (j + 1) * rows_dev] * row_hot[...]
            hx[i * group + j] = jnp.sum(part, axis=0, keepdims=True)
        return carry

    lax.fori_loop(0, mem_loc // group, forecast, 0)

    def a_copy(src, dst, peer):
        return pltpu.make_async_remote_copy(
            src_ref=hx.at[src],
            dst_ref=a_in.at[dst],
            send_sem=a_send.at[peer],
            recv_sem=a_recv.at[dst],
            device_id=(e, peer),
            device_id_type=MESH,
        )

    def a_start(i, carry):
        peer = lax.rem(d + i, dom_n)
        a_copy(peer, d, peer).start()
        return carry

    def a_wait(i, carry):
        peer = lax.rem(d + i, dom_n)
        a_copy(peer, peer, peer).wait_recv()
        return carry

    lax.fori_loop(1, dom_n, a_start, 0)
    a_in[d] = hx[d]

    half = rows_dev * mem_loc // 2
    counts = {
        (0, 0): ens_n // 2,
        (1, 0): (ens_n - 1) // 2,
        (0, 1): (ens_n - 1) // 2,
        (1, 1): ens_n // 2,
    }

    def g_copy(way, part, step, arriving):
        shift = step + 1 if arriving else step
        block = lax.rem(e - shift + ens_n, ens_n) if way == 0 else lax.rem(e + shift, ens_n)
        peer = lax.rem(e + 1, ens_n) if way == 0 else lax.rem(e + ens_n - 1, ens_n)
        where = full.at[block, pl.ds(part * half, half), :]
        slot = (way * 2 + part) * (ens_n // 2) + step
        return pltpu.make_async_remote_copy(
            src_ref=where,
            dst_ref=where,
            send_sem=g_send.at[slot],
            recv_sem=g_recv.at[slot],
            device_id=(peer, d),
            device_id_type=MESH,
        )

    g_started = []

    def g_start(part, step):
        for way in (0, 1):
            if step > 0 and step - 1 < counts[way, part]:
                g_copy(way, part, step - 1, True).wait_recv()
            if step < counts[way, part]:
                g_copy(way, part, step, False).start()
                g_started.append((way, part, step))

    services = [(p, s) for s in range(1, ens_n // 2 + 1) for p in (0, 1)]

    def service():
        if services:
            g_start(*services.pop(0))

    lax.fori_loop(1, dom_n, a_wait, 0)

    for b in range(nb):
        row = a_in[own_s[b]]
        for p in range(parts):
            piece = row[:, p * cols : (p + 1) * cols]
            b_out[b, p] = piece
            c_src[b, p, pl.ds(e, 1), :] = piece

    def b_copy(slot, peer):
        return pltpu.make_async_remote_copy(
            src_ref=b_out,
            dst_ref=c_src.at[:, :, pl.ds(slot, 1), :],
            send_sem=b_send.at[peer],
            recv_sem=b_recv.at[slot],
            device_id=(peer, d),
            device_id_type=MESH,
        )

    def b_start(i, carry):
        peer = lax.rem(e + i, ens_n)
        b_copy(e, peer).start()
        return carry

    def b_wait(i, carry):
        peer = lax.rem(e + i, ens_n)
        b_copy(peer, peer).wait_recv()
        return carry

    lax.fori_loop(1, ens_n, b_start, 0)
    g_start(0, 0)
    g_start(1, 0)
    lax.fori_loop(1, ens_n, b_wait, 0)

    spans = ((0, 1), (1, nb - 1))

    def c_copy(part, slot, peer):
        first, count = spans[part]
        return pltpu.make_async_remote_copy(
            src_ref=c_src.at[pl.ds(first, count)],
            dst_ref=arrived.at[
                pl.ds(first, count), :, pl.ds(pl.multiple_of(slot * ens_n, ens_n), ens_n), :
            ],
            send_sem=c_send.at[part * dom_n + peer],
            recv_sem=c_recv.at[part * dom_n + slot],
            device_id=(e, peer),
            device_id_type=MESH,
        )

    def c_start(part):
        def one(i, carry):
            peer = lax.rem(d + i, dom_n)
            c_copy(part, d, peer).start()
            return carry

        lax.fori_loop(1, dom_n, one, 0)

    def c_wait(part):
        def one(i, carry):
            peer = lax.rem(d + i, dom_n)
            c_copy(part, peer, peer).wait_recv()
            return carry

        lax.fori_loop(1, dom_n, one, 0)

    c_start(0)
    c_start(1)
    arrived[:, :, pl.ds(pl.multiple_of(d * ens_n, ens_n), ens_n), :] = c_src[...]
    service()
    c_wait(0)
    service()

    def in_order(b):
        columns = [
            jnp.concatenate(
                [arrived.at[b, p][pl.ds(k, mem_loc, stride=ens_n), :] for k in range(ens_n)], axis=0
            )
            for p in range(parts)
        ]
        return jnp.concatenate(columns, axis=1)

    eye = (
        lax.broadcasted_iota(jnp.int32, (members, members), 0)
        == lax.broadcasted_iota(jnp.int32, (members, members), 1)
    ).astype(jnp.float32)
    scale = 1.0 / (members - 1.0)
    low = members + PAD

    def analyse(observed, b):
        ybar = jnp.sum(observed, axis=0, keepdims=True) * (1.0 / members)
        rs = 1.0 / jnp.sqrt(var[pl.ds(b, 1), :])
        anom = (observed - ybar) * rs
        innov = (obs[pl.ds(b, 1), :] - ybar) * rs
        left = jnp.concatenate([anom, jnp.broadcast_to(innov, (PAD, nob))], axis=0)
        both = dot_nt(left, anom) * scale
        gram = both[:members]
        z = both[members:]
        size = 1.001 * jnp.sqrt(jnp.sum(gram * gram, keepdims=True))
        alpha = 2.0 / (2.0 + size)
        r = size / (2.0 + size)
        k_mat = eye + gram
        err = eye - alpha * k_mat
        a = 2.0 / (2.0 - r * r)
        first = a * alpha
        pair[:members] = first * (eye + err)
        pair[members:low] = first * (z + dot(z, err))
        pair[low:] = a * dot(err, err) - (a - 1.0) * eye

        def step(i, r):
            a = 2.0 / (2.0 - r * r)
            held = pair[...]
            prod = dot(held, held[low:])
            pair[:low] = a * (held[:low] + prod[:low])
            pair[low:] = a * prod[low:] - (a - 1.0) * eye
            return a - 1.0

        r = lax.fori_loop(0, 7, step, a - 1.0)
        a = 2.0 / (2.0 - r * r)
        x = pair[:low]
        x = a * (x + dot(x, pair[low:]))
        for _ in range(2):
            x = x + dot(x, eye - dot(k_mat, x[:members]))
        return x

    def update(x, columns):
        prod = dot(x, columns)
        return 0.5 * (columns + prod[:members]) + prod[members : members + 1]

    observed = in_order(0)
    for b in range(nb):
        x = analyse(observed, b)
        service()
        if b == 0:
            c_wait(1)
            total[...] = 0.5 * (eye + x[:members]) + x[members : members + 1]
            for later in range(1, nb):
                fresh = update(x, in_order(later))
                if later == 1:
                    observed = fresh
                else:
                    prior[later] = fresh
        elif b < nb - 1:
            for later in range(b + 1, nb):
                fresh = update(x, prior[later])
                if later == b + 1:
                    observed = fresh
                else:
                    prior[later] = fresh
            total[...] = update(x, total[...])
        else:
            pair[:low] = x
            rows = pl.ds(pl.multiple_of(e * mem_loc, mem_loc), mem_loc)
            thin = jnp.concatenate([pair[rows], x[members:]], axis=0)
            prod = dot(thin, total[...])
            t_own[...] = (
                0.5 * (total[rows] + prod[:mem_loc]) + prod[mem_loc : mem_loc + 1]
            )

    while services:
        service()

    hi, lo = split2(t_own[...])
    both = jnp.concatenate([hi, lo], axis=0)

    def apply(i, carry):
        pieces = [
            jnp.concatenate(
                [
                    full[k, pl.ds(pl.multiple_of((2 * i + j) * mem_loc, mem_loc), mem_loc), :]
                    for k in range(ens_n)
                ],
                axis=0,
            )
            for j in range(2)
        ]
        x_hi, x_lo = split2(jnp.concatenate(pieces, axis=1))
        one = bdot(both, x_hi)
        res = one[:mem_loc] + one[mem_loc:] + bdot(hi, x_lo)
        out[pl.ds(2 * i, mem_loc, stride=rows_dev), :] = res[:, :cols]
        out[pl.ds(2 * i + 1, mem_loc, stride=rows_dev), :] = res[:, cols:]
        return carry

    lax.fori_loop(0, rows_dev // 2, apply, 0)

    for copy in halos:
        copy.wait_send()
    for way, part, step in g_started:
        g_copy(way, part, step, False).wait_send()

    def sent_dom(i, carry):
        peer = lax.rem(d + i, dom_n)
        a_copy(peer, d, peer).wait_send()
        c_copy(0, d, peer).wait_send()
        c_copy(1, d, peer).wait_send()
        return carry

    def sent_ens(i, carry):
        b_copy(e, lax.rem(e + i, ens_n)).wait_send()
        return carry

    lax.fori_loop(1, dom_n, sent_dom, 0)
    lax.fori_loop(1, ens_n, sent_ens, 0)


def on_device(mesh_shape, state, row_c, col_c, diff, obs, var, off, owners):
    ens_n, dom_n = mesh_shape
    mem_loc, rows_dev, cols = state.shape
    members = mem_loc * ens_n
    nb, nob = obs.shape
    high = rows_dev + 2 * HALO
    f32 = jnp.float32
    sem = pltpu.SemaphoreType.DMA
    slots = 4 * (ens_n // 2)
    hbm = pl.BlockSpec(memory_space=pl.ANY)
    vmem = pl.BlockSpec(memory_space=pltpu.VMEM)
    result = pl.pallas_call(
        kernel,
        out_shape=jax.ShapeDtypeStruct((mem_loc * rows_dev, cols), f32),
        in_specs=[hbm, hbm, hbm, hbm, vmem, vmem, vmem, vmem, pl.BlockSpec(memory_space=pltpu.SMEM)],
        out_specs=vmem,
        scratch_shapes=[
            pltpu.VMEM((mem_loc, high, cols), f32),
            pltpu.VMEM((3, high, cols), f32),
            pltpu.VMEM((ens_n, rows_dev * mem_loc, cols), f32),
            pltpu.VMEM((cols, nob), jnp.bfloat16),
            pltpu.VMEM((rows_dev, nob), f32),
            pltpu.VMEM((mem_loc, 1, nob), f32),
            pltpu.VMEM((dom_n, 1, nob), f32),
            pltpu.VMEM((nb, nob // cols, 1, cols), f32),
            pltpu.VMEM((nb, nob // cols, ens_n, cols), f32),
            pltpu.VMEM((nb, nob // cols, members, cols), f32),
            pltpu.VMEM((nb, members, nob), f32),
            pltpu.VMEM((2 * members + PAD, members), f32),
            pltpu.VMEM((members, members), f32),
            pltpu.VMEM((mem_loc, members), f32),
            sem((4,)),
            sem((8,)),
            sem((8,)),
            sem((dom_n,)),
            sem((dom_n,)),
            sem((ens_n,)),
            sem((ens_n,)),
            sem((2 * dom_n,)),
            sem((2 * dom_n,)),
            sem((slots,)),
            sem((slots,)),
        ],
        compiler_params=pltpu.CompilerParams(
            collective_id=0, has_side_effects=True, vmem_limit_bytes=48 * 1024 * 1024
        ),
    )(state, row_c, col_c, diff, obs, var, off, owners.reshape(nb, 1), owners)
    return result.reshape(mem_loc, rows_dev, cols)


def solution(mesh):
    sizes = (mesh.shape["ens"], mesh.shape["dom"])
    return jax.shard_map(
        functools.partial(on_device, sizes),
        mesh=mesh,
        in_specs=(
            P("ens", "dom", None),
            P("dom", None),
            P("dom", None),
            P("dom", None),
            P(),
            P(),
            P(),
            P(),
        ),
        out_specs=P("ens", "dom", None),
        check_vma=False,
    )
```

time: 602 us -> 101 us (0.17); the launches traced: 594 us -> 101 us
  other arithmetic: 236 us -> 0 us
  waiting for transfers between devices: 234 us -> 0 us
  Pallas kernels: 0 us -> 94.1 us
  starting transfers between devices: 27 us -> 0 us
  blocking collectives: 24.1 us -> 0 us
  between operations: 22.3 us -> 0.02 us
  local copies, waits for them, and re-layouts: 29 us -> 6.77 us
  matrix products: 21.7 us -> 0 us
    another operation x37 -> x0, other arithmetic: 227 us -> none  [the longest x28 139 us: on_device(): factor = jnp.linalg.cholesky(system)]
    psum x4 -> x0, waiting for transfers between devices: 220 us -> none  [over_axes(): return functools.reduce(lax.psum, axes, x)]
    pallas_call x0 -> x1, Pallas kernels: none -> 94.1 us  [on_device(): pl.pallas_call(kernel, out_shape=jax.ShapeDtypeStruct((mem_loc * rows_dev...]
    all_to_all x1 -> x0, blocking collectives: 24.1 us -> none  [on_device(): return lax.all_to_all(back, 'ens', split_axis=0, concat_axis=1, tiled=True)]
    ppermute x8 -> x0, starting transfers between devices: 20.1 us -> none  [the longest x4 16.2 us: with_halo(): after = lax.ppermute(leading, axis, down)]
    another operation x37 -> x0, local copies, waits for them, and re-layouts: 16.3 us -> none  [the longest x29 16.2 us: on_device(): weights = jax.scipy.linalg.cho_solve((factor, True), target.T).T]
    dot_general x24 -> x0, matrix products: 13 us -> none  [the longest x14 7.5 us: contract_members(): lax.dot_general(left_side, right_side, (((0,), (0,)), ((), ())), precisio...]
    all_to_all x1 -> x0, waiting for transfers between devices: 11.9 us -> none  [on_device(): lax.all_to_all(field, 'ens', split_axis=1, concat_axis=0, tiled=True)]
  transfers between devices with their start and end apart: 13 -> 0, of which waited for: 11 -> 0; matrix products, arithmetic and copies ran while one was open for 0% -> 0% of each run, Pallas kernels for 0% -> 0%
where the time goes in v1:
time: 101 us
  Pallas kernels  94.1 us (93%)
  local copies, waits for them, and re-layouts  6.77 us (7%)
    pallas_call x1, Pallas kernels, on_device(): pl.pallas_call(kernel, out_shape=jax.ShapeDtypeStruct((mem_loc * rows_dev...  94.1 us
    unnamed x17, local copies, waits for them, and re-layouts  6.02 us

profile of v1, /device:TPU:1, one launch (start us, length us, event | category | flops | bytes accessed | tf_op | source)
XLA Modules:
  0.0 100.9 jit_solution(638399231876792741)
XLA Ops:
  0.0 0.0 copy-start.4
  0.0 0.8 copy.9.own_v
  0.8 0.0 copy-done.4
  0.8 0.0 copy-start
  0.8 1.0 %copy-done = f32[32,32,128]{2,1,0:T(8,128)S(1)} copy-done((f32[32,32,128]{2,1,0:T(8,128)S(1)}, f32[32,32,128]{2,1,0:T(8,128)}, u32[]{:S(2)}) %copy-start) | copy-done | bytes 524312
  1.8 0.0 copy-start.1
  1.8 0.7 copy-done.1
  2.5 0.0 copy-start.2
  2.5 0.7 copy-done.2
  3.2 0.0 copy-start.3
  3.2 0.7 copy-done.3
  4.0 0.0 copy-start.5
  4.0 0.7 copy-done.5
  4.6 0.0 copy-start.6
  4.6 0.7 copy-done.6
  5.3 0.0 copy-start.7
  5.3 0.7 copy-done.7
  6.0 94.1 %shard_map.82 = f32[1024,128]{1,0:T(8,128)S(1)} custom-call(f32[32,32,128]{2,1,0:T(8,128)S(1)} %copy-done, f32[32,128]{1,0:T(8,128)S(1)} %copy-done.1, f32[32,128]{1,0:T(8,128)S(1)} %copy-done.2, f32[32,128]{1,0:T(8,128)S(1)} %copy-done.3, f32[4,256]{1,0:T(4,128)S(1)} %copy-done.4, f32[4,256]{1,0:T(4,128)S(1)} %copy-done.5, s32[4,256]{1,0:T(4,128)S(1)} %copy-done.6, ...), custom_call_target="tpu_custom_call" | custom-call | tf_op jit(solution)/shard_map/pallas_call | solution.py:442
  100.1 0.8 copy.11
Async XLA Ops:
  0.0 0.8 copy-start.4
  0.8 1.0 %copy-start = (f32[32,32,128]{2,1,0:T(8,128)S(1)}, f32[32,32,128]{2,1,0:T(8,128)}, u32[]{:S(2)}) copy-start(f32[32,32,128]{2,1,0:T(8,128)} %state.1) | copy-start | bytes 1572868
  1.8 0.7 copy-start.1
  2.5 0.7 copy-start.2
  3.2 0.7 copy-start.3
  4.0 0.7 copy-start.5
  4.6 0.7 copy-start.6
  5.3 0.7 copy-start.7

commit v2 on v1

--- a/solution.py
+++ b/solution.py
@@ -30,23 +30,23 @@
     return hi, lo
 
 
-def split3(x):
-    hi = x.astype(jnp.bfloat16)
-    rest = x - hi.astype(jnp.float32)
-    mid = rest.astype(jnp.bfloat16)
-    lo = (rest - mid.astype(jnp.float32)).astype(jnp.bfloat16)
-    return hi, mid, lo
-
-
 def bdot(a, b):
     return jnp.dot(a, b, preferred_element_type=jnp.float32)
 
 
+def dot3(a, b):
+    a_hi, a_lo = a
+    b_hi, b_lo = b
+    return bdot(
+        jnp.concatenate([a_hi, a_lo, a_hi], axis=1), jnp.concatenate([b_hi, b_hi, b_lo], axis=0)
+    )
+
+
 def kernel(
-    state, row_c, col_c, diff, obs, var, off, own_v, own_s, out,
-    ext, cext, full, lane_hot, row_hot, hx, a_in, b_out, c_src, arrived, prior, pair,
-    total, t_own, load_sem, h_send, h_recv, a_send, a_recv, b_send, b_recv,
-    c_send, c_recv, g_send, g_recv,
+    state, row_c, col_c, diff, obs_in, var_in, off_in, own_in, out,
+    ext, cext, cells, weight, full, obs, var, off, own, lane_hot, row_hot, hx, a_in, b_out, c_src,
+    arrived, prior, pair, gram_s, total, t_own,
+    load_sem, h_send, h_recv, a_send, a_recv, b_send, b_recv, c_send, c_recv, g_send, g_recv,
 ):
     ens_n = lax.axis_size("ens")
     dom_n = lax.axis_size("dom")
@@ -56,14 +56,13 @@
     members = mem_loc * ens_n
     nb, nob = obs.shape
     parts = nob // cols
-
-    loads = [
-        pltpu.make_async_copy(state, ext.at[:, pl.ds(HALO, rows_dev), :], load_sem.at[0])
-    ]
-    for i, coef in enumerate((row_c, col_c, diff)):
-        loads.append(
-            pltpu.make_async_copy(coef, cext.at[i, pl.ds(HALO, rows_dev), :], load_sem.at[1 + i])
-        )
+    high = rows_dev + 2 * HALO
+
+    inner = pl.ds(HALO, rows_dev)
+    moves = [(state, ext.at[:, inner, :])]
+    moves += [(coef, cext.at[i, inner, :]) for i, coef in enumerate((row_c, col_c, diff))]
+    moves += [(obs_in, obs), (var_in, var), (off_in, off), (own_in, own)]
+    loads = [pltpu.make_async_copy(src, dst, load_sem.at[i]) for i, (src, dst) in enumerate(moves)]
     for copy in loads:
         copy.start()
 
@@ -115,8 +114,12 @@
     for copy in halos:
         copy.start()
 
-    mine = (own_v[...] == d).astype(jnp.int32)
-    offs = jnp.sum(off[...] * mine, axis=0, keepdims=True)
+    for copy in loads:
+        copy.wait()
+
+    offs = jnp.zeros((1, nob), jnp.int32)
+    for b in range(nb):
+        offs = offs + off[pl.ds(b, 1), :] * (own[b] == d).astype(jnp.int32)
     lane_of = lax.rem(offs, cols)
     row_of = lax.div(offs, cols)
     lane_hot[...] = (
@@ -126,79 +129,63 @@
         lax.broadcasted_iota(jnp.int32, (rows_dev, nob), 0) == row_of
     ).astype(jnp.float32)
 
-    for copy in loads:
-        copy.wait()
+    def turn(first, count):
+        def one(m, carry):
+            cells[pl.ds(first * mem_loc + m, count, stride=mem_loc), :] = ext[m, pl.ds(first, count), :]
+            return carry
+
+        lax.fori_loop(0, mem_loc, one, 0, unroll=4)
+
+    turn(HALO, rows_dev)
     for copy in halos:
         copy.wait_recv()
-
-    high = rows_dev + 2 * HALO
+    turn(0, HALO)
+    turn(HALO + rows_dev, HALO)
     rc, cc, df = cext[0], cext[1], cext[2]
-    w_up = rc + df
-    w_left = cc + df
-    w_mid = 1.0 - rc - cc - 4.0 * df
-    group = 2
-
-    def forecast(i, carry):
-        fields = []
-        for j in range(group):
-            m = i * group + j
-            x = ext[m]
-            for _ in range(FSTEPS):
-                above = pltpu.roll(x, 1, 0)
-                below = pltpu.roll(x, high - 1, 0)
-                left = pltpu.roll(x, 1, 1)
-                right = pltpu.roll(x, cols - 1, 1)
-                x = w_mid * x + w_up * above + w_left * left + df * (below + right)
-            x = x[HALO : HALO + rows_dev]
-            full[e, pl.ds(m, rows_dev, stride=mem_loc), :] = x
-            fields.append(x)
-        hi, mid, lo = split3(jnp.concatenate(fields, axis=0))
-        hot = lane_hot[...]
-        picked = bdot(hi, hot) + bdot(mid, hot) + bdot(lo, hot)
-        for j in range(group):
-            part = picked[j * rows_dev : (j + 1) * rows_dev] * row_hot[...]
-            hx[i * group + j] = jnp.sum(part, axis=0, keepdims=True)
-        return carry
-
-    lax.fori_loop(0, mem_loc // group, forecast, 0)
-
-    def a_copy(src, dst, peer):
-        return pltpu.make_async_remote_copy(
-            src_ref=hx.at[src],
-            dst_ref=a_in.at[dst],
-            send_sem=a_send.at[peer],
-            recv_sem=a_recv.at[dst],
-            device_id=(e, peer),
-            device_id_type=MESH,
-        )
-
-    def a_start(i, carry):
-        peer = lax.rem(d + i, dom_n)
-        a_copy(peer, d, peer).start()
-        return carry
-
-    def a_wait(i, carry):
-        peer = lax.rem(d + i, dom_n)
-        a_copy(peer, peer, peer).wait_recv()
-        return carry
-
-    lax.fori_loop(1, dom_n, a_start, 0)
-    a_in[d] = hx[d]
+    weight[0] = 1.0 - rc - cc - 4.0 * df
+    weight[1] = rc + df
+    weight[2] = cc + df
+    weight[3] = df
+
+    def at_row(r):
+        return pl.ds(pl.multiple_of(r * mem_loc, mem_loc), mem_loc)
+
+    def coef(i, r):
+        return jnp.broadcast_to(weight[i, pl.ds(r, 1), :], (mem_loc, cols))
+
+    for step in range(FSTEPS):
+        first = HALO - (FSTEPS - 1 - step)
+        last = HALO + rows_dev + (FSTEPS - 1 - step)
+
+        def one(r, carry, step=step):
+            above, here = carry
+            below = cells[at_row(r + 1), :]
+            left = pltpu.roll(here, 1, 1)
+            right = pltpu.roll(here, cols - 1, 1)
+            fresh = (
+                coef(0, r) * here
+                + coef(1, r) * above
+                + coef(2, r) * left
+                + coef(3, r) * (below + right)
+            )
+            if step < FSTEPS - 1:
+                cells[at_row(r), :] = fresh
+            else:
+                full[e, at_row(r - HALO), :] = fresh
+            return here, below
+
+        lax.fori_loop(
+            first, last, one, (cells[at_row(first - 1), :], cells[at_row(first), :]), unroll=4
+        )
 
     half = rows_dev * mem_loc // 2
-    counts = {
-        (0, 0): ens_n // 2,
-        (1, 0): (ens_n - 1) // 2,
-        (0, 1): (ens_n - 1) // 2,
-        (1, 1): ens_n // 2,
-    }
 
     def g_copy(way, part, step, arriving):
         shift = step + 1 if arriving else step
         block = lax.rem(e - shift + ens_n, ens_n) if way == 0 else lax.rem(e + shift, ens_n)
         peer = lax.rem(e + 1, ens_n) if way == 0 else lax.rem(e + ens_n - 1, ens_n)
-        where = full.at[block, pl.ds(part * half, half), :]
-        slot = (way * 2 + part) * (ens_n // 2) + step
+        where = full.at[block, pl.ds(pl.multiple_of(part * half, half), half), :]
+        slot = (way * 2 + part) * 4 + step
         return pltpu.make_async_remote_copy(
             src_ref=where,
             dst_ref=where,
@@ -208,26 +195,60 @@
             device_id_type=MESH,
         )
 
-    g_started = []
-
     def g_start(part, step):
         for way in (0, 1):
-            if step > 0 and step - 1 < counts[way, part]:
-                g_copy(way, part, step - 1, True).wait_recv()
-            if step < counts[way, part]:
-                g_copy(way, part, step, False).start()
-                g_started.append((way, part, step))
-
-    services = [(p, s) for s in range(1, ens_n // 2 + 1) for p in (0, 1)]
-
-    def service():
-        if services:
-            g_start(*services.pop(0))
+            g_copy(way, part, step, False).start()
+
+    def g_wait(part, step):
+        for way in (0, 1):
+            g_copy(way, part, step, True).wait_recv()
+
+    g_start(0, 0)
+
+    rows_once = 4
+
+    def pick(i, acc):
+        block = pl.ds(pl.multiple_of(i * rows_once * mem_loc, rows_once * mem_loc), rows_once * mem_loc)
+        hi, lo = split2(full[e, block, :])
+        hot = lane_hot[...]
+        picked = bdot(hi, hot) + bdot(lo, hot)
+        for j in range(rows_once):
+            acc = acc + picked[j * mem_loc : (j + 1) * mem_loc] * row_hot[
+                pl.ds(i * rows_once + j, 1), :
+            ]
+        return acc
+
+    hx[...] = lax.fori_loop(
+        0, rows_dev // rows_once, pick, jnp.zeros((mem_loc, nob), jnp.float32), unroll=2
+    )
+
+    def a_copy(src, dst, peer):
+        return pltpu.make_async_remote_copy(
+            src_ref=hx.at[pl.ds(src, 1), :],
+            dst_ref=a_in.at[dst],
+            send_sem=a_send.at[peer],
+            recv_sem=a_recv.at[dst],
+            device_id=(e, peer),
+            device_id_type=MESH,
+        )
+
+    def a_start(i, carry):
+        peer = lax.rem(d + i, dom_n)
+        a_copy(peer, d, peer).start()
+        return carry
+
+    def a_wait(i, carry):
+        peer = lax.rem(d + i, dom_n)
+        a_copy(peer, peer, peer).wait_recv()
+        return carry
+
+    lax.fori_loop(1, dom_n, a_start, 0)
+    a_in[d] = hx[pl.ds(d, 1), :]
 
     lax.fori_loop(1, dom_n, a_wait, 0)
 
     for b in range(nb):
-        row = a_in[own_s[b]]
+        row = a_in[own[b]]
         for p in range(parts):
             piece = row[:, p * cols : (p + 1) * cols]
             b_out[b, p] = piece
@@ -254,7 +275,6 @@
         return carry
 
     lax.fori_loop(1, ens_n, b_start, 0)
-    g_start(0, 0)
     g_start(1, 0)
     lax.fori_loop(1, ens_n, b_wait, 0)
 
@@ -291,10 +311,12 @@
 
     c_start(0)
     c_start(1)
+    g_wait(0, 0)
+    g_start(0, 1)
     arrived[:, :, pl.ds(pl.multiple_of(d * ens_n, ens_n), ens_n), :] = c_src[...]
-    service()
     c_wait(0)
-    service()
+    g_wait(1, 0)
+    g_start(1, 1)
 
     def in_order(b):
         columns = [
@@ -325,17 +347,20 @@
         alpha = 2.0 / (2.0 + size)
         r = size / (2.0 + size)
         k_mat = eye + gram
+        gram_s[...] = k_mat
         err = eye - alpha * k_mat
         a = 2.0 / (2.0 - r * r)
+        prod = dot(jnp.concatenate([z, err], axis=0), err)
         first = a * alpha
         pair[:members] = first * (eye + err)
-        pair[members:low] = first * (z + dot(z, err))
-        pair[low:] = a * dot(err, err) - (a - 1.0) * eye
+        pair[members:low] = first * (z + prod[:PAD])
+        pair[low:] = a * prod[PAD:] - (a - 1.0) * eye
 
         def step(i, r):
             a = 2.0 / (2.0 - r * r)
             held = pair[...]
-            prod = dot(held, held[low:])
+            hi, lo = split2(held)
+            prod = dot3((hi, lo), (hi[low:], lo[low:]))
             pair[:low] = a * (held[:low] + prod[:low])
             pair[low:] = a * prod[low:] - (a - 1.0) * eye
             return a - 1.0
@@ -343,47 +368,58 @@
         r = lax.fori_loop(0, 7, step, a - 1.0)
         a = 2.0 / (2.0 - r * r)
         x = pair[:low]
-        x = a * (x + dot(x, pair[low:]))
-        for _ in range(2):
-            x = x + dot(x, eye - dot(k_mat, x[:members]))
-        return x
+        x = a * (x + dot3(split2(x), split2(pair[low:])))
+        pair[:low] = x
+
+        def correct(i, carry):
+            x = pair[:low]
+            rest = eye - dot(gram_s[...], x[:members])
+            pair[:low] = x + dot3(split2(x), split2(rest))
+            return carry
+
+        lax.fori_loop(0, 2, correct, 0)
+        x = pair[:low]
+        want = (lax.broadcasted_iota(jnp.int32, (low, 1), 0) < members).astype(jnp.float32)
+        return x + (want - jnp.sum(x, axis=1, keepdims=True)) * (1.0 / members)
 
     def update(x, columns):
-        prod = dot(x, columns)
+        prod = dot3(x, split2(columns))
         return 0.5 * (columns + prod[:members]) + prod[members : members + 1]
 
-    observed = in_order(0)
-    for b in range(nb):
-        x = analyse(observed, b)
-        service()
-        if b == 0:
+    prior[0] = in_order(0)
+    total[...] = eye
+
+    def batch(b, carry):
+        x = split2(analyse(prior[b], b))
+
+        @pl.when(b == 0)
+        def _():
             c_wait(1)
-            total[...] = 0.5 * (eye + x[:members]) + x[members : members + 1]
             for later in range(1, nb):
-                fresh = update(x, in_order(later))
-                if later == 1:
-                    observed = fresh
-                else:
-                    prior[later] = fresh
-        elif b < nb - 1:
-            for later in range(b + 1, nb):
-                fresh = update(x, prior[later])
-                if later == b + 1:
-                    observed = fresh
-                else:
-                    prior[later] = fresh
-            total[...] = update(x, total[...])
-        else:
-            pair[:low] = x
-            rows = pl.ds(pl.multiple_of(e * mem_loc, mem_loc), mem_loc)
-            thin = jnp.concatenate([pair[rows], x[members:]], axis=0)
-            prod = dot(thin, total[...])
-            t_own[...] = (
-                0.5 * (total[rows] + prod[:mem_loc]) + prod[mem_loc : mem_loc + 1]
-            )
-
-    while services:
-        service()
+                prior[later] = in_order(later)
+
+        def later_one(later, carry):
+            prior[later] = update(x, prior[later])
+            return carry
+
+        lax.fori_loop(b + 1, nb, later_one, 0)
+        total[...] = update(x, total[...])
+        part = lax.rem(b, 2)
+        step = 2 + lax.div(b, 2)
+        g_wait(part, step - 1)
+        for way in (0, 1):
+
+            @pl.when((b < 2) | (part == way))
+            def _():
+                g_copy(way, part, step, False).start()
+
+        return carry
+
+    lax.fori_loop(0, nb, batch, 0)
+    rows = pl.ds(pl.multiple_of(e * mem_loc, mem_loc), mem_loc)
+    t_own[...] = total[rows, :]
+    g_copy(0, 0, 3, True).wait_recv()
+    g_copy(1, 1, 3, True).wait_recv()
 
     hi, lo = split2(t_own[...])
     both = jnp.concatenate([hi, lo], axis=0)
@@ -410,8 +446,10 @@
 
     for copy in halos:
         copy.wait_send()
-    for way, part, step in g_started:
-        g_copy(way, part, step, False).wait_send()
+    for way in (0, 1):
+        for part in (0, 1):
+            for step in range(4 if way == part else 3):
+                g_copy(way, part, step, False).wait_send()
 
     def sent_dom(i, carry):
         peer = lax.rem(d + i, dom_n)
@@ -436,21 +474,27 @@
     high = rows_dev + 2 * HALO
     f32 = jnp.float32
     sem = pltpu.SemaphoreType.DMA
-    slots = 4 * (ens_n // 2)
+    assert ens_n == 8 and nb == 4
     hbm = pl.BlockSpec(memory_space=pl.ANY)
     vmem = pl.BlockSpec(memory_space=pltpu.VMEM)
     result = pl.pallas_call(
         kernel,
         out_shape=jax.ShapeDtypeStruct((mem_loc * rows_dev, cols), f32),
-        in_specs=[hbm, hbm, hbm, hbm, vmem, vmem, vmem, vmem, pl.BlockSpec(memory_space=pltpu.SMEM)],
+        in_specs=[hbm] * 8,
         out_specs=vmem,
         scratch_shapes=[
             pltpu.VMEM((mem_loc, high, cols), f32),
             pltpu.VMEM((3, high, cols), f32),
+            pltpu.VMEM((high * mem_loc, cols), f32),
+            pltpu.VMEM((4, high, cols), f32),
             pltpu.VMEM((ens_n, rows_dev * mem_loc, cols), f32),
+            pltpu.VMEM((nb, nob), f32),
+            pltpu.VMEM((nb, nob), f32),
+            pltpu.VMEM((nb, nob), jnp.int32),
+            pltpu.SMEM((nb,), jnp.int32),
             pltpu.VMEM((cols, nob), jnp.bfloat16),
             pltpu.VMEM((rows_dev, nob), f32),
-            pltpu.VMEM((mem_loc, 1, nob), f32),
+            pltpu.VMEM((mem_loc, nob), f32),
             pltpu.VMEM((dom_n, 1, nob), f32),
             pltpu.VMEM((nb, nob // cols, 1, cols), f32),
             pltpu.VMEM((nb, nob // cols, ens_n, cols), f32),
@@ -458,8 +502,9 @@
             pltpu.VMEM((nb, members, nob), f32),
             pltpu.VMEM((2 * members + PAD, members), f32),
             pltpu.VMEM((members, members), f32),
+            pltpu.VMEM((members, members), f32),
             pltpu.VMEM((mem_loc, members), f32),
-            sem((4,)),
+            sem((8,)),
             sem((8,)),
             sem((8,)),
             sem((dom_n,)),
@@ -468,13 +513,13 @@
             sem((ens_n,)),
             sem((2 * dom_n,)),
             sem((2 * dom_n,)),
-            sem((slots,)),
-            sem((slots,)),
+            sem((16,)),
+            sem((16,)),
         ],
         compiler_params=pltpu.CompilerParams(
-            collective_id=0, has_side_effects=True, vmem_limit_bytes=48 * 1024 * 1024
+            collective_id=0, has_side_effects=True, vmem_limit_bytes=60 * 1024 * 1024
         ),
-    )(state, row_c, col_c, diff, obs, var, off, owners.reshape(nb, 1), owners)
+    )(state, row_c, col_c, diff, obs, var, off, owners)
     return result.reshape(mem_loc, rows_dev, cols)
 
 

time: 101 us -> 85.8 us (0.85)
  Pallas kernels: 94.1 us -> 83.8 us
  local copies, waits for them, and re-layouts: 6.77 us -> 1.87 us
    pallas_call x1, Pallas kernels: 94.1 us -> 83.8 us  [on_device(): pl.pallas_call(kernel, out_shape=jax.ShapeDtypeStruct((mem_loc * rows_dev...]
    unnamed x17 -> x1, local copies, waits for them, and re-layouts: 6.02 us -> 1.87 us
where the time goes in v2:
time: 85.8 us; the launch traced here: 85.7 us
  Pallas kernels  83.8 us (98%)
  local copies, waits for them, and re-layouts  1.87 us (2%)
    pallas_call x1, Pallas kernels, on_device(): pl.pallas_call(kernel, out_shape=jax.ShapeDtypeStruct((mem_loc * rows_dev...  83.8 us
    unnamed x1, local copies, waits for them, and re-layouts  1.87 us

profile of v2, /device:TPU:1, one launch (start us, length us, event | category | flops | bytes accessed | tf_op | source)
XLA Modules:
  0.0 85.7 jit_solution(16128391266558445479)
XLA Ops:
  0.0 83.8 %shard_map.82 = f32[1024,128]{1,0:T(8,128)} custom-call(f32[32,32,128]{2,1,0:T(8,128)} %state.1, f32[32,128]{1,0:T(8,128)} %row_c.1, f32[32,128]{1,0:T(8,128)} %col_c.1, f32[32,128]{1,0:T(8,128)} %diff.1, f32[4,256]{1,0:T(4,128)} %obs_in.1, f32[4,256]{1,0:T(4,128)} %var_in.1, s32[4,256]{1,0:T(4,128)} %off_in.1, s32[4]{0:T(128)} %own_in.1), custom_call_target="tpu_custom_call" | custom-call | tf_op jit(solution)/shard_map/pallas_call | solution.py:480
  83.8 1.9 %copy.10 = f32[32,32,128]{2,1,0:T(8,128)} copy(f32[32,32,128]{2,1,0:T(8,128)} %bitcast.1) | data formatting | bytes 1048576

commit v3 on v2

--- a/solution.py
+++ b/solution.py
@@ -44,7 +44,7 @@
 
 def kernel(
     state, row_c, col_c, diff, obs_in, var_in, off_in, own_in, out,
-    ext, cext, cells, weight, full, obs, var, off, own, lane_hot, row_hot, hx, a_in, b_out, c_src,
+    ext, cext, cells, other, weight, full, obs, var, off, own, lane_hot, row_hot, hx, a_in, b_out, c_src,
     arrived, prior, pair, gram_s, total, t_own,
     load_sem, h_send, h_recv, a_send, a_recv, b_send, b_recv, c_send, c_recv, g_send, g_recv,
 ):
@@ -82,6 +82,8 @@
 
     lax.fori_loop(1, dom_n, greet_dom, 0)
     lax.fori_loop(1, ens_n, greet_ens, 0)
+    for copy in loads:
+        copy.wait()
     pl.semaphore_wait(barrier, dom_n - 1 + ens_n - 1)
 
     down = lax.rem(d + 1, dom_n)
@@ -92,7 +94,7 @@
     ):
         halos.append(
             pltpu.make_async_remote_copy(
-                src_ref=state.at[:, pl.ds(src_row, HALO), :],
+                src_ref=ext.at[:, pl.ds(HALO + src_row, HALO), :],
                 dst_ref=ext.at[:, pl.ds(dst_row, HALO), :],
                 send_sem=h_send.at[way * 4],
                 recv_sem=h_recv.at[way * 4],
@@ -100,10 +102,10 @@
                 device_id_type=MESH,
             )
         )
-        for i, coef in enumerate((row_c, col_c, diff)):
+        for i in range(3):
             halos.append(
                 pltpu.make_async_remote_copy(
-                    src_ref=coef.at[pl.ds(src_row, HALO), :],
+                    src_ref=cext.at[i, pl.ds(HALO + src_row, HALO), :],
                     dst_ref=cext.at[i, pl.ds(dst_row, HALO), :],
                     send_sem=h_send.at[way * 4 + 1 + i],
                     recv_sem=h_recv.at[way * 4 + 1 + i],
@@ -113,9 +115,6 @@
             )
     for copy in halos:
         copy.start()
-
-    for copy in loads:
-        copy.wait()
 
     offs = jnp.zeros((1, nob), jnp.int32)
     for b in range(nb):
@@ -157,9 +156,11 @@
         first = HALO - (FSTEPS - 1 - step)
         last = HALO + rows_dev + (FSTEPS - 1 - step)
 
-        def one(r, carry, step=step):
+        src, dst = (cells, other) if step % 2 == 0 else (other, cells)
+
+        def one(r, carry, step=step, src=src, dst=dst):
             above, here = carry
-            below = cells[at_row(r + 1), :]
+            below = src[at_row(r + 1), :]
             left = pltpu.roll(here, 1, 1)
             right = pltpu.roll(here, cols - 1, 1)
             fresh = (
@@ -169,13 +170,13 @@
                 + coef(3, r) * (below + right)
             )
             if step < FSTEPS - 1:
-                cells[at_row(r), :] = fresh
+                dst[at_row(r), :] = fresh
             else:
                 full[e, at_row(r - HALO), :] = fresh
             return here, below
 
         lax.fori_loop(
-            first, last, one, (cells[at_row(first - 1), :], cells[at_row(first), :]), unroll=4
+            first, last, one, (src[at_row(first - 1), :], src[at_row(first), :]), unroll=4
         )
 
     half = rows_dev * mem_loc // 2
@@ -355,30 +356,30 @@
         pair[:members] = first * (eye + err)
         pair[members:low] = first * (z + prod[:PAD])
         pair[low:] = a * prod[PAD:] - (a - 1.0) * eye
-
-        def step(i, r):
+        r = a - 1.0
+
+        def advance(r, held, prod):
             a = 2.0 / (2.0 - r * r)
-            held = pair[...]
-            hi, lo = split2(held)
-            prod = dot3((hi, lo), (hi[low:], lo[low:]))
             pair[:low] = a * (held[:low] + prod[:low])
             pair[low:] = a * prod[low:] - (a - 1.0) * eye
             return a - 1.0
 
-        r = lax.fori_loop(0, 7, step, a - 1.0)
+        held = pair[...]
+        r = advance(r, held, dot(held, held[low:]))
+
+        def step(i, r):
+            held = pair[...]
+            hi, lo = split2(held)
+            return advance(r, held, dot3((hi, lo), (hi[low:], lo[low:])))
+
+        r = lax.fori_loop(0, 3, step, r)
+        serve(b, 0)
+        r = lax.fori_loop(3, 6, step, r)
         a = 2.0 / (2.0 - r * r)
         x = pair[:low]
         x = a * (x + dot3(split2(x), split2(pair[low:])))
-        pair[:low] = x
-
-        def correct(i, carry):
-            x = pair[:low]
-            rest = eye - dot(gram_s[...], x[:members])
-            pair[:low] = x + dot3(split2(x), split2(rest))
-            return carry
-
-        lax.fori_loop(0, 2, correct, 0)
-        x = pair[:low]
+        rest = eye - dot(gram_s[...], x[:members])
+        x = x + dot3(split2(x), split2(rest))
         want = (lax.broadcasted_iota(jnp.int32, (low, 1), 0) < members).astype(jnp.float32)
         return x + (want - jnp.sum(x, axis=1, keepdims=True)) * (1.0 / members)
 
@@ -387,37 +388,54 @@
         return 0.5 * (columns + prod[:members]) + prod[members : members + 1]
 
     prior[0] = in_order(0)
-    total[...] = eye
+
+    def serve(b, place):
+        @pl.when(b < 2)
+        def _():
+            step = 2 + b
+            g_wait(place, step - 1)
+            for way in (0, 1):
+
+                @pl.when((b < 1) | (place == way))
+                def _():
+                    g_copy(way, place, step, False).start()
+
+    rows = pl.ds(pl.multiple_of(e * mem_loc, mem_loc), mem_loc)
 
     def batch(b, carry):
-        x = split2(analyse(prior[b], b))
+        x = analyse(prior[b], b)
+        serve(b, 1)
+        x2 = split2(x)
 
         @pl.when(b == 0)
         def _():
+            total[...] = 0.5 * (eye + x[:members]) + x[members : members + 1]
             c_wait(1)
             for later in range(1, nb):
                 prior[later] = in_order(later)
 
         def later_one(later, carry):
-            prior[later] = update(x, prior[later])
+            prior[later] = update(x2, prior[later])
             return carry
 
         lax.fori_loop(b + 1, nb, later_one, 0)
-        total[...] = update(x, total[...])
-        part = lax.rem(b, 2)
-        step = 2 + lax.div(b, 2)
-        g_wait(part, step - 1)
-        for way in (0, 1):
-
-            @pl.when((b < 2) | (part == way))
-            def _():
-                g_copy(way, part, step, False).start()
+
+        @pl.when((b > 0) & (b < nb - 1))
+        def _():
+            total[...] = update(x2, total[...])
+
+        @pl.when(b == nb - 1)
+        def _():
+            pair[:low] = x
+            thin = jnp.concatenate([pair[rows, :], x[members:]], axis=0)
+            prod = dot3(split2(thin), split2(total[...]))
+            t_own[...] = (
+                0.5 * (total[rows, :] + prod[:mem_loc]) + prod[mem_loc : mem_loc + 1]
+            )
 
         return carry
 
     lax.fori_loop(0, nb, batch, 0)
-    rows = pl.ds(pl.multiple_of(e * mem_loc, mem_loc), mem_loc)
-    t_own[...] = total[rows, :]
     g_copy(0, 0, 3, True).wait_recv()
     g_copy(1, 1, 3, True).wait_recv()
 
@@ -442,7 +460,7 @@
         out[pl.ds(2 * i + 1, mem_loc, stride=rows_dev), :] = res[:, cols:]
         return carry
 
-    lax.fori_loop(0, rows_dev // 2, apply, 0)
+    lax.fori_loop(0, rows_dev // 2, apply, 0, unroll=2)
 
     for copy in halos:
         copy.wait_send()
@@ -485,6 +503,7 @@
         scratch_shapes=[
             pltpu.VMEM((mem_loc, high, cols), f32),
             pltpu.VMEM((3, high, cols), f32),
+            pltpu.VMEM((high * mem_loc, cols), f32),
             pltpu.VMEM((high * mem_loc, cols), f32),
             pltpu.VMEM((4, high, cols), f32),
             pltpu.VMEM((ens_n, rows_dev * mem_loc, cols), f32),

time: 85.8 us -> 80.9 us (0.943)
  Pallas kernels: 83.8 us -> 78.8 us
    pallas_call x1, Pallas kernels: 83.8 us -> 78.8 us  [on_device(): pl.pallas_call(kernel, out_shape=jax.ShapeDtypeStruct((mem_loc * rows_dev...]
where the time goes in v3:
time: 80.9 us; the launch traced here: 80.7 us
  Pallas kernels  78.8 us (97%)
  local copies, waits for them, and re-layouts  1.87 us (2%)
    pallas_call x1, Pallas kernels, on_device(): pl.pallas_call(kernel, out_shape=jax.ShapeDtypeStruct((mem_loc * rows_dev...  78.8 us
    unnamed x1, local copies, waits for them, and re-layouts  1.87 us

profile of v3, /device:TPU:1, one launch (start us, length us, event | category | flops | bytes accessed | tf_op | source)
XLA Modules:
  0.0 80.7 jit_solution(17903509541550706759)
XLA Ops:
  0.0 78.8 %shard_map.82 = f32[1024,128]{1,0:T(8,128)} custom-call(f32[32,32,128]{2,1,0:T(8,128)} %state.1, f32[32,128]{1,0:T(8,128)} %row_c.1, f32[32,128]{1,0:T(8,128)} %col_c.1, f32[32,128]{1,0:T(8,128)} %diff.1, f32[4,256]{1,0:T(4,128)} %obs_in.1, f32[4,256]{1,0:T(4,128)} %var_in.1, s32[4,256]{1,0:T(4,128)} %off_in.1, s32[4]{0:T(128)} %own_in.1), custom_call_target="tpu_custom_call" | custom-call | tf_op jit(solution)/shard_map/pallas_call | solution.py:498
  78.9 1.9 %copy.10 = f32[32,32,128]{2,1,0:T(8,128)} copy(f32[32,32,128]{2,1,0:T(8,128)} %bitcast.1) | data formatting | bytes 1048576

commit v4 on v3

--- a/solution.py
+++ b/solution.py
@@ -11,23 +11,31 @@
 FSTEPS = 4
 HALO = 8
 PAD = 8
-HIGHEST = lax.Precision.HIGHEST
-
-
-def dot(a, b, precision=HIGHEST):
-    return jnp.dot(a, b, precision=precision, preferred_element_type=jnp.float32)
-
-
-def dot_nt(a, b):
-    return lax.dot_general(
-        a, b, (((1,), (1,)), ((), ())), precision=HIGHEST, preferred_element_type=jnp.float32
-    )
 
 
 def split2(x):
     hi = x.astype(jnp.bfloat16)
     lo = (x - hi.astype(jnp.float32)).astype(jnp.bfloat16)
     return hi, lo
+
+
+def dot6(a, b, transposed=False):
+    a_hi, a_mid, a_lo = a
+    b_hi, b_mid, b_lo = b
+    axis = 1 if transposed else 0
+    left = jnp.concatenate([a_hi, a_mid, a_hi, a_mid, a_lo, a_hi], axis=1)
+    right = jnp.concatenate([b_hi, b_hi, b_mid, b_mid, b_hi, b_lo], axis=axis)
+    return lax.dot_general(
+        left, right, (((1,), (axis,)), ((), ())), preferred_element_type=jnp.float32
+    )
+
+
+def split3(x):
+    hi = x.astype(jnp.bfloat16)
+    rest = x - hi.astype(jnp.float32)
+    mid = rest.astype(jnp.bfloat16)
+    lo = (rest - mid.astype(jnp.float32)).astype(jnp.bfloat16)
+    return hi, mid, lo
 
 
 def bdot(a, b):
@@ -176,7 +184,11 @@
             return here, below
 
         lax.fori_loop(
-            first, last, one, (src[at_row(first - 1), :], src[at_row(first), :]), unroll=4
+            first,
+            last,
+            one,
+            (src[at_row(first - 1), :], src[at_row(first), :]),
+            unroll=(last - first) // 2,
         )
 
     half = rows_dev * mem_loc // 2
@@ -340,8 +352,8 @@
         rs = 1.0 / jnp.sqrt(var[pl.ds(b, 1), :])
         anom = (observed - ybar) * rs
         innov = (obs[pl.ds(b, 1), :] - ybar) * rs
-        left = jnp.concatenate([anom, jnp.broadcast_to(innov, (PAD, nob))], axis=0)
-        both = dot_nt(left, anom) * scale
+        left = split3(jnp.concatenate([anom, jnp.broadcast_to(innov, (PAD, nob))], axis=0))
+        both = dot6(left, [piece[:members] for piece in left], True) * scale
         gram = both[:members]
         z = both[members:]
         size = 1.001 * jnp.sqrt(jnp.sum(gram * gram, keepdims=True))
@@ -351,12 +363,12 @@
         gram_s[...] = k_mat
         err = eye - alpha * k_mat
         a = 2.0 / (2.0 - r * r)
-        prod = dot(jnp.concatenate([z, err], axis=0), err)
         first = a * alpha
         pair[:members] = first * (eye + err)
+        hi, lo = split2(jnp.concatenate([z, err], axis=0))
+        prod = dot3((hi, lo), (hi[PAD:], lo[PAD:]))
         pair[members:low] = first * (z + prod[:PAD])
         pair[low:] = a * prod[PAD:] - (a - 1.0) * eye
-        r = a - 1.0
 
         def advance(r, held, prod):
             a = 2.0 / (2.0 - r * r)
@@ -364,21 +376,21 @@
             pair[low:] = a * prod[low:] - (a - 1.0) * eye
             return a - 1.0
 
-        held = pair[...]
-        r = advance(r, held, dot(held, held[low:]))
-
         def step(i, r):
             held = pair[...]
             hi, lo = split2(held)
             return advance(r, held, dot3((hi, lo), (hi[low:], lo[low:])))
 
-        r = lax.fori_loop(0, 3, step, r)
-        serve(b, 0)
-        r = lax.fori_loop(3, 6, step, r)
+        r = lax.fori_loop(0, 4, step, a - 1.0)
+        serve(b)
+        r = lax.fori_loop(4, 7, step, r)
         a = 2.0 / (2.0 - r * r)
         x = pair[:low]
         x = a * (x + dot3(split2(x), split2(pair[low:])))
-        rest = eye - dot(gram_s[...], x[:members])
+        x2 = split2(x)
+        rest = eye - dot3(split2(gram_s[...]), (x2[0][:members], x2[1][:members]))
+        x = x + dot3(x2, split2(rest))
+        rest = eye - dot6(split3(gram_s[...]), split3(x[:members]))
         x = x + dot3(split2(x), split2(rest))
         want = (lax.broadcasted_iota(jnp.int32, (low, 1), 0) < members).astype(jnp.float32)
         return x + (want - jnp.sum(x, axis=1, keepdims=True)) * (1.0 / members)
@@ -389,22 +401,20 @@
 
     prior[0] = in_order(0)
 
-    def serve(b, place):
-        @pl.when(b < 2)
-        def _():
-            step = 2 + b
-            g_wait(place, step - 1)
-            for way in (0, 1):
-
-                @pl.when((b < 1) | (place == way))
-                def _():
-                    g_copy(way, place, step, False).start()
+    def serve(b):
+        part = lax.rem(b, 2)
+        step = 2 + lax.div(b, 2)
+        g_wait(part, step - 1)
+        for way in (0, 1):
+
+            @pl.when((b < 2) | (part == way))
+            def _():
+                g_copy(way, part, step, False).start()
 
     rows = pl.ds(pl.multiple_of(e * mem_loc, mem_loc), mem_loc)
 
     def batch(b, carry):
         x = analyse(prior[b], b)
-        serve(b, 1)
         x2 = split2(x)
 
         @pl.when(b == 0)
@@ -437,7 +447,6 @@
 
     lax.fori_loop(0, nb, batch, 0)
     g_copy(0, 0, 3, True).wait_recv()
-    g_copy(1, 1, 3, True).wait_recv()
 
     hi, lo = split2(t_own[...])
     both = jnp.concatenate([hi, lo], axis=0)
@@ -460,7 +469,9 @@
         out[pl.ds(2 * i + 1, mem_loc, stride=rows_dev), :] = res[:, cols:]
         return carry
 
-    lax.fori_loop(0, rows_dev // 2, apply, 0, unroll=2)
+    lax.fori_loop(0, rows_dev // 4, apply, 0, unroll=4)
+    g_copy(1, 1, 3, True).wait_recv()
+    lax.fori_loop(rows_dev // 4, rows_dev // 2, apply, 0, unroll=4)
 
     for copy in halos:
         copy.wait_send()

time: 80.9 us -> 76.4 us (0.944)
  Pallas kernels: 78.8 us -> 74.3 us
    pallas_call x1, Pallas kernels: 78.8 us -> 74.3 us  [on_device(): pl.pallas_call(kernel, out_shape=jax.ShapeDtypeStruct((mem_loc * rows_dev...]
where the time goes in v4:
time: 76.4 us; the launch traced here: 76.2 us
  Pallas kernels  74.3 us (97%)
  local copies, waits for them, and re-layouts  1.87 us (2%)
    pallas_call x1, Pallas kernels, on_device(): pl.pallas_call(kernel, out_shape=jax.ShapeDtypeStruct((mem_loc * rows_dev...  74.3 us
    unnamed x1, local copies, waits for them, and re-layouts  1.87 us

profile of v4, /device:TPU:1, one launch (start us, length us, event | category | flops | bytes accessed | tf_op | source)
XLA Modules:
  0.0 76.2 jit_solution(10141136313640886772)
XLA Ops:
  0.0 74.3 %shard_map.82 = f32[1024,128]{1,0:T(8,128)} custom-call(f32[32,32,128]{2,1,0:T(8,128)} %state.1, f32[32,128]{1,0:T(8,128)} %row_c.1, f32[32,128]{1,0:T(8,128)} %col_c.1, f32[32,128]{1,0:T(8,128)} %diff.1, f32[4,256]{1,0:T(4,128)} %obs_in.1, f32[4,256]{1,0:T(4,128)} %var_in.1, s32[4,256]{1,0:T(4,128)} %off_in.1, s32[4]{0:T(128)} %own_in.1), custom_call_target="tpu_custom_call" | custom-call | tf_op jit(solution)/shard_map/pallas_call | solution.py:509
  74.4 1.9 %copy.10 = f32[32,32,128]{2,1,0:T(8,128)} copy(f32[32,32,128]{2,1,0:T(8,128)} %bitcast.1) | data formatting | bytes 1048576

commit v5 on v4

--- a/solution.py
+++ b/solution.py
@@ -235,11 +235,11 @@
         0, rows_dev // rows_once, pick, jnp.zeros((mem_loc, nob), jnp.float32), unroll=2
     )
 
-    def a_copy(src, dst, peer):
+    def a_copy(src, dst, peer, turn_at):
         return pltpu.make_async_remote_copy(
             src_ref=hx.at[pl.ds(src, 1), :],
             dst_ref=a_in.at[dst],
-            send_sem=a_send.at[peer],
+            send_sem=a_send.at[turn_at],
             recv_sem=a_recv.at[dst],
             device_id=(e, peer),
             device_id_type=MESH,
@@ -247,12 +247,12 @@
 
     def a_start(i, carry):
         peer = lax.rem(d + i, dom_n)
-        a_copy(peer, d, peer).start()
+        a_copy(peer, d, peer, i).start()
         return carry
 
     def a_wait(i, carry):
         peer = lax.rem(d + i, dom_n)
-        a_copy(peer, peer, peer).wait_recv()
+        a_copy(peer, peer, peer, i).wait_recv()
         return carry
 
     lax.fori_loop(1, dom_n, a_start, 0)
@@ -267,11 +267,11 @@
             b_out[b, p] = piece
             c_src[b, p, pl.ds(e, 1), :] = piece
 
-    def b_copy(slot, peer):
+    def b_copy(slot, peer, turn_at):
         return pltpu.make_async_remote_copy(
             src_ref=b_out,
             dst_ref=c_src.at[:, :, pl.ds(slot, 1), :],
-            send_sem=b_send.at[peer],
+            send_sem=b_send.at[turn_at],
             recv_sem=b_recv.at[slot],
             device_id=(peer, d),
             device_id_type=MESH,
@@ -279,12 +279,12 @@
 
     def b_start(i, carry):
         peer = lax.rem(e + i, ens_n)
-        b_copy(e, peer).start()
+        b_copy(e, peer, i).start()
         return carry
 
     def b_wait(i, carry):
         peer = lax.rem(e + i, ens_n)
-        b_copy(peer, peer).wait_recv()
+        b_copy(peer, peer, i).wait_recv()
         return carry
 
     lax.fori_loop(1, ens_n, b_start, 0)
@@ -293,14 +293,14 @@
 
     spans = ((0, 1), (1, nb - 1))
 
-    def c_copy(part, slot, peer):
+    def c_copy(part, slot, peer, turn_at):
         first, count = spans[part]
         return pltpu.make_async_remote_copy(
             src_ref=c_src.at[pl.ds(first, count)],
             dst_ref=arrived.at[
                 pl.ds(first, count), :, pl.ds(pl.multiple_of(slot * ens_n, ens_n), ens_n), :
             ],
-            send_sem=c_send.at[part * dom_n + peer],
+            send_sem=c_send.at[part * dom_n + turn_at],
             recv_sem=c_recv.at[part * dom_n + slot],
             device_id=(e, peer),
             device_id_type=MESH,
@@ -309,7 +309,7 @@
     def c_start(part):
         def one(i, carry):
             peer = lax.rem(d + i, dom_n)
-            c_copy(part, d, peer).start()
+            c_copy(part, d, peer, i).start()
             return carry
 
         lax.fori_loop(1, dom_n, one, 0)
@@ -317,7 +317,7 @@
     def c_wait(part):
         def one(i, carry):
             peer = lax.rem(d + i, dom_n)
-            c_copy(part, peer, peer).wait_recv()
+            c_copy(part, peer, peer, i).wait_recv()
             return carry
 
         lax.fori_loop(1, dom_n, one, 0)
@@ -327,6 +327,19 @@
     g_wait(0, 0)
     g_start(0, 1)
     arrived[:, :, pl.ds(pl.multiple_of(d * ens_n, ens_n), ens_n), :] = c_src[...]
+    for copy in halos:
+        copy.wait_send()
+
+    def sent_a(i, carry):
+        a_copy(0, d, down, i).wait_send()
+        return carry
+
+    def sent_b(i, carry):
+        b_copy(e, lax.rem(e + 1, ens_n), i).wait_send()
+        return carry
+
+    lax.fori_loop(1, dom_n, sent_a, 0, unroll=True)
+    lax.fori_loop(1, ens_n, sent_b, 0, unroll=True)
     c_wait(0)
     g_wait(1, 0)
     g_start(1, 1)
@@ -383,14 +396,17 @@
 
         r = lax.fori_loop(0, 4, step, a - 1.0)
         serve(b)
-        r = lax.fori_loop(4, 7, step, r)
+        r = lax.fori_loop(4, 6, step, r)
         a = 2.0 / (2.0 - r * r)
         x = pair[:low]
         x = a * (x + dot3(split2(x), split2(pair[low:])))
+        r = a - 1.0
+        a = 2.0 / (2.0 - r * r)
+        k_parts = split3(gram_s[...])
         x2 = split2(x)
-        rest = eye - dot3(split2(gram_s[...]), (x2[0][:members], x2[1][:members]))
-        x = x + dot3(x2, split2(rest))
-        rest = eye - dot6(split3(gram_s[...]), split3(x[:members]))
+        rest = eye - dot3(k_parts[:2], (x2[0][:members], x2[1][:members]))
+        x = a * (x + dot3(x2, split2(rest)))
+        rest = eye - dot6(k_parts, split3(x[:members]))
         x = x + dot3(split2(x), split2(rest))
         want = (lax.broadcasted_iota(jnp.int32, (low, 1), 0) < members).astype(jnp.float32)
         return x + (want - jnp.sum(x, axis=1, keepdims=True)) * (1.0 / members)
@@ -473,26 +489,17 @@
     g_copy(1, 1, 3, True).wait_recv()
     lax.fori_loop(rows_dev // 4, rows_dev // 2, apply, 0, unroll=4)
 
-    for copy in halos:
-        copy.wait_send()
     for way in (0, 1):
         for part in (0, 1):
             for step in range(4 if way == part else 3):
                 g_copy(way, part, step, False).wait_send()
 
-    def sent_dom(i, carry):
-        peer = lax.rem(d + i, dom_n)
-        a_copy(peer, d, peer).wait_send()
-        c_copy(0, d, peer).wait_send()
-        c_copy(1, d, peer).wait_send()
-        return carry
-
-    def sent_ens(i, carry):
-        b_copy(e, lax.rem(e + i, ens_n)).wait_send()
-        return carry
-
-    lax.fori_loop(1, dom_n, sent_dom, 0)
-    lax.fori_loop(1, ens_n, sent_ens, 0)
+    def sent_c(i, carry):
+        c_copy(0, d, down, i).wait_send()
+        c_copy(1, d, down, i).wait_send()
+        return carry
+
+    lax.fori_loop(1, dom_n, sent_c, 0, unroll=True)
 
 
 def on_device(mesh_shape, state, row_c, col_c, diff, obs, var, off, owners):

time: 76.4 us -> 74.9 us (0.980)
  Pallas kernels: 74.3 us -> 72.8 us
    pallas_call x1, Pallas kernels: 74.3 us -> 72.8 us  [on_device(): pl.pallas_call(kernel, out_shape=jax.ShapeDtypeStruct((mem_loc * rows_dev...]
where the time goes in v5:
time: 74.9 us; the launch traced here: 74.7 us
  Pallas kernels  72.8 us (97%)
  local copies, waits for them, and re-layouts  1.87 us (2%)
    pallas_call x1, Pallas kernels, on_device(): pl.pallas_call(kernel, out_shape=jax.ShapeDtypeStruct((mem_loc * rows_dev...  72.8 us
    unnamed x1, local copies, waits for them, and re-layouts  1.87 us

profile of v5, /device:TPU:1, one launch (start us, length us, event | category | flops | bytes accessed | tf_op | source)
XLA Modules:
  0.0 74.7 jit_solution(11126469992371251816)
XLA Ops:
  0.0 72.8 %shard_map.82 = f32[1024,128]{1,0:T(8,128)} custom-call(f32[32,32,128]{2,1,0:T(8,128)} %state.1, f32[32,128]{1,0:T(8,128)} %row_c.1, f32[32,128]{1,0:T(8,128)} %col_c.1, f32[32,128]{1,0:T(8,128)} %diff.1, f32[4,256]{1,0:T(4,128)} %obs_in.1, f32[4,256]{1,0:T(4,128)} %var_in.1, s32[4,256]{1,0:T(4,128)} %off_in.1, s32[4]{0:T(128)} %own_in.1), custom_call_target="tpu_custom_call" | custom-call | tf_op jit(solution)/shard_map/pallas_call | solution.py:516
  72.8 1.9 %copy.10 = f32[32,32,128]{2,1,0:T(8,128)} copy(f32[32,32,128]{2,1,0:T(8,128)} %bitcast.1) | data formatting | bytes 1048576

commit v6 on v5

--- a/solution.py
+++ b/solution.py
@@ -255,7 +255,7 @@
         a_copy(peer, peer, peer, i).wait_recv()
         return carry
 
-    lax.fori_loop(1, dom_n, a_start, 0)
+    lax.fori_loop(1, dom_n, a_start, 0, unroll=True)
     a_in[d] = hx[pl.ds(d, 1), :]
 
     lax.fori_loop(1, dom_n, a_wait, 0)
@@ -287,7 +287,7 @@
         b_copy(peer, peer, i).wait_recv()
         return carry
 
-    lax.fori_loop(1, ens_n, b_start, 0)
+    lax.fori_loop(1, ens_n, b_start, 0, unroll=True)
     g_start(1, 0)
     lax.fori_loop(1, ens_n, b_wait, 0)
 
@@ -312,7 +312,7 @@
             c_copy(part, d, peer, i).start()
             return carry
 
-        lax.fori_loop(1, dom_n, one, 0)
+        lax.fori_loop(1, dom_n, one, 0, unroll=True)
 
     def c_wait(part):
         def one(i, carry):
@@ -394,9 +394,8 @@
             hi, lo = split2(held)
             return advance(r, held, dot3((hi, lo), (hi[low:], lo[low:])))
 
-        r = lax.fori_loop(0, 4, step, a - 1.0)
         serve(b)
-        r = lax.fori_loop(4, 6, step, r)
+        r = lax.fori_loop(0, 6, step, a - 1.0)
         a = 2.0 / (2.0 - r * r)
         x = pair[:low]
         x = a * (x + dot3(split2(x), split2(pair[low:])))

time: 74.9 us -> 73 us (0.975)
  Pallas kernels: 72.8 us -> 71 us
    pallas_call x1, Pallas kernels: 72.8 us -> 71 us  [on_device(): pl.pallas_call(kernel, out_shape=jax.ShapeDtypeStruct((mem_loc * rows_dev...]
where the time goes in v6:
time: 73 us; the launch traced here: 72.9 us
  Pallas kernels  71 us (97%)
  local copies, waits for them, and re-layouts  1.87 us (3%)
    pallas_call x1, Pallas kernels, on_device(): pl.pallas_call(kernel, out_shape=jax.ShapeDtypeStruct((mem_loc * rows_dev...  71 us
    unnamed x1, local copies, waits for them, and re-layouts  1.87 us

profile of v6, /device:TPU:1, one launch (start us, length us, event | category | flops | bytes accessed | tf_op | source)
XLA Modules:
  0.0 72.9 jit_solution(15624222866025926162)
XLA Ops:
  0.0 71.0 %shard_map.82 = f32[1024,128]{1,0:T(8,128)} custom-call(f32[32,32,128]{2,1,0:T(8,128)} %state.1, f32[32,128]{1,0:T(8,128)} %row_c.1, f32[32,128]{1,0:T(8,128)} %col_c.1, f32[32,128]{1,0:T(8,128)} %diff.1, f32[4,256]{1,0:T(4,128)} %obs_in.1, f32[4,256]{1,0:T(4,128)} %var_in.1, s32[4,256]{1,0:T(4,128)} %off_in.1, s32[4]{0:T(128)} %own_in.1), custom_call_target="tpu_custom_call" | custom-call | tf_op jit(solution)/shard_map/pallas_call | solution.py:515
  71.0 1.9 %copy.10 = f32[32,32,128]{2,1,0:T(8,128)} copy(f32[32,32,128]{2,1,0:T(8,128)} %bitcast.1) | data formatting | bytes 1048576

commit v7 on v6

--- a/solution.py
+++ b/solution.py
@@ -258,7 +258,7 @@
     lax.fori_loop(1, dom_n, a_start, 0, unroll=True)
     a_in[d] = hx[pl.ds(d, 1), :]
 
-    lax.fori_loop(1, dom_n, a_wait, 0)
+    lax.fori_loop(1, dom_n, a_wait, 0, unroll=True)
 
     for b in range(nb):
         row = a_in[own[b]]
@@ -289,7 +289,7 @@
 
     lax.fori_loop(1, ens_n, b_start, 0, unroll=True)
     g_start(1, 0)
-    lax.fori_loop(1, ens_n, b_wait, 0)
+    lax.fori_loop(1, ens_n, b_wait, 0, unroll=True)
 
     spans = ((0, 1), (1, nb - 1))
 
@@ -320,7 +320,7 @@
             c_copy(part, peer, peer, i).wait_recv()
             return carry
 
-        lax.fori_loop(1, dom_n, one, 0)
+        lax.fori_loop(1, dom_n, one, 0, unroll=True)
 
     c_start(0)
     c_start(1)

time: 73 us -> 72.3 us (level)
  no operation moved by 1% of the time
where the time goes in v7:
time: 72.3 us; the launch traced here: 72.2 us
  Pallas kernels  70.3 us (97%)
  local copies, waits for them, and re-layouts  1.87 us (3%)
    pallas_call x1, Pallas kernels, on_device(): pl.pallas_call(kernel, out_shape=jax.ShapeDtypeStruct((mem_loc * rows_dev...  70.3 us
    unnamed x1, local copies, waits for them, and re-layouts  1.87 us

profile of v7, /device:TPU:1, one launch (start us, length us, event | category | flops | bytes accessed | tf_op | source)
XLA Modules:
  0.0 72.2 jit_solution(8476727572905519772)
XLA Ops:
  0.0 70.3 %shard_map.82 = f32[1024,128]{1,0:T(8,128)} custom-call(f32[32,32,128]{2,1,0:T(8,128)} %state.1, f32[32,128]{1,0:T(8,128)} %row_c.1, f32[32,128]{1,0:T(8,128)} %col_c.1, f32[32,128]{1,0:T(8,128)} %diff.1, f32[4,256]{1,0:T(4,128)} %obs_in.1, f32[4,256]{1,0:T(4,128)} %var_in.1, s32[4,256]{1,0:T(4,128)} %off_in.1, s32[4]{0:T(128)} %own_in.1), custom_call_target="tpu_custom_call" | custom-call | tf_op jit(solution)/shard_map/pallas_call | solution.py:515
  70.3 1.9 %copy.10 = f32[32,32,128]{2,1,0:T(8,128)} copy(f32[32,32,128]{2,1,0:T(8,128)} %bitcast.1) | data formatting | bytes 1048576
